TPU v7x, 32 devices: a whole 2x2x4 slice. The times are simulated.
32 devices in a mesh: dev: 32 (over z, y, x, core).
Axes of the slice: x: 2, y: 2, z: 4, core: 2. Of those that a mesh axis runs over, the one named last changes fastest.
Arguments:
- ensemble: float32 [128, 4, 256, 256], P('dev'), may hold values from -6 to 6
- flow_speed: float32 [2, 256, 256], replicated, may hold values from -0.6 to 0.6
- spreading_coefficient: float32 [4, 256, 256], replicated, may hold values from 0.01 to 0.12
- obs_values: float32 [2, 4096], replicated, may hold values from -6 to 6
- obs_var: float32 [4096], replicated, may hold values from 0.02 to 0.5
- obs_block: int32 [4096], replicated, may hold values from 0 to 16383, as said below
- readers: int32 [128, 128], replicated, may hold values from 0 to 4095, as said below
- counts: int32 [128], replicated, may hold values from 32 to 128
Outputs:
- analysed: float32 [128, 4, 256, 256], P('dev')
Inputs may be any that keep to these rules, and one draw needn't show every extreme that they name: `obs_block`: observations are ordered by block row: observation i lies in block row (i * 64) // 4096. `readers`: each row lists distinct observations, mostly within three block rows of the patch; slots at or past the patch's count hold valid indices and are not read.
All inputs are finite; a program needn't handle non-finite values.
Results may differ from a plain program's by a relative error of at most 0.0003.
Values sent between devices are 32-bit elements; how exact they have to be, the bound alone decides.
No kernel may reach another device: no remote copies, remote signals or barrier semaphores. Data moves between devices by JAX's collectives and lax.ppermute only.
A program may use at most 320 MiB of HBM per device.

v0:
```python
import jax
import jax.numpy as jnp
from jax import lax
from jax.sharding import PartitionSpec as P

V = 4
NX = 256
NY = 256
PR = 2
BLOCK = 4
STEPS = 3
CYCLES = 2
NS_ITERS = 10


EXACT_DOT = lax.Precision.HIGHEST
TAPER_ROWS = 6.0


def tendency(sample_ensemble, flow_speed, spreading_coefficient):
    shifted_up = jnp.roll(sample_ensemble, -1, axis=-2)
    shifted_down = jnp.roll(sample_ensemble, 1, axis=-2)
    shifted_left = jnp.roll(sample_ensemble, -1, axis=-1)
    shifted_right = jnp.roll(sample_ensemble, 1, axis=-1)
    advect_fields = (
        flow_speed[0] * (shifted_up - shifted_down) * 0.5
        + flow_speed[1] * (shifted_left - shifted_right) * 0.5
    )
    return (
        spreading_coefficient
        * (shifted_up + shifted_down + shifted_left + shifted_right - 4.0 * sample_ensemble)
        - advect_fields
    )


def prior_guess(sample_ensemble, flow_speed, spreading_coefficient):
    for step in range(STEPS):
        section_one = sample_ensemble + tendency(sample_ensemble, flow_speed, spreading_coefficient)
        section_two = 0.75 * sample_ensemble + 0.25 * (
            section_one + tendency(section_one, flow_speed, spreading_coefficient)
        )
        sample_ensemble = sample_ensemble / 3.0 + 2.0 / 3.0 * (
            section_two + tendency(section_two, flow_speed, spreading_coefficient)
        )
    return sample_ensemble


def block_means(sample_ensemble):
    lead = sample_ensemble.shape[:-2]
    rows_sum = sample_ensemble.reshape(lead + (NX // BLOCK, BLOCK, NY)).sum(-2)
    column = jnp.arange(NY, dtype=jnp.int32) // BLOCK
    target_state = jnp.arange(NY // BLOCK, dtype=jnp.int32)
    pooling_matrix = (column[:, None] == target_state[None, :]).astype(jnp.float32)
    pooled = jnp.einsum("...c,cb->...b", rows_sum, pooling_matrix, precision=EXACT_DOT)
    return pooled.reshape(sample_ensemble.shape[0], -1) / (BLOCK * BLOCK)


def obs_weights(patch_index, chosen, obs_count, obs_block, obs_var):
    obs_blocks = obs_block[chosen]
    block_row = obs_blocks // (NY // BLOCK) % (NX // BLOCK)
    obs_row = block_row.astype(jnp.float32) * BLOCK + 0.5 * (BLOCK - 1)
    patch_row = patch_index.astype(jnp.float32) * PR + 0.5 * (PR - 1)
    row_gap = jnp.abs(obs_row - patch_row[..., None])
    distance = jnp.minimum(row_gap, NX - row_gap)
    taper = jnp.exp(-0.5 * (distance / TAPER_ROWS) ** 2)
    slot_index = jnp.arange(chosen.shape[-1], dtype=jnp.int32)
    in_list = slot_index < obs_count[..., None]
    return jnp.where(in_list, taper / obs_var[chosen], jnp.zeros_like(taper))


def analyse(patches, obs_rows, sensor_readings, weights):
    members = patches.shape[0]
    patch_count = obs_rows.shape[1]
    shaped = patches.reshape(members, patches.shape[1], patch_count, PR, patches.shape[3])
    mean_state = shaped.mean(0)
    pert = shaped - mean_state
    hx_mean = obs_rows.mean(0)
    ypert = obs_rows - hx_mean
    innovation = sensor_readings - hx_mean
    identity = jnp.eye(members, dtype=jnp.float32)
    gram_matrix = jnp.einsum("mpj,pj,npj->pmn", ypert, weights, ypert, precision=EXACT_DOT) / (
        members - 1
    )
    system = identity + gram_matrix
    entrywise_magnitude = jnp.sqrt(jnp.sum(system * system, axis=(1, 2)))
    root_up = system / entrywise_magnitude[:, None, None]
    inv_root = jnp.broadcast_to(identity, system.shape)

    def sweep_once(sweep, carry):
        root_up, inv_root = carry
        newton = 1.5 * identity - 0.5 * jnp.einsum(
            "pij,pjk->pik", inv_root, root_up, precision=EXACT_DOT
        )
        root_next = jnp.einsum("pij,pjk->pik", root_up, newton, precision=EXACT_DOT)
        inv_next = jnp.einsum("pij,pjk->pik", newton, inv_root, precision=EXACT_DOT)
        return (root_next, inv_next)

    root_up, inv_root = lax.fori_loop(0, NS_ITERS, sweep_once, (root_up, inv_root))
    obs_drive = jnp.einsum("mpj,pj->pm", ypert, weights * innovation, precision=EXACT_DOT) / (
        members - 1
    )
    inner = jnp.einsum("pij,pj->pi", inv_root, obs_drive, precision=EXACT_DOT)
    mean_w = (
        jnp.einsum("pij,pj->pi", inv_root, inner, precision=EXACT_DOT)
        / entrywise_magnitude[:, None]
    )
    transform = inv_root / jnp.sqrt(entrywise_magnitude)[:, None, None] + mean_w[:, :, None]
    updated = mean_state + jnp.einsum("kvprn,pkm->mvprn", pert, transform, precision=EXACT_DOT)
    return updated.reshape(patches.shape)


def local(
    ensemble, flow_speed, spreading_coefficient, obs_values, obs_var, obs_block, readers, counts
):
    sample_ensemble = ensemble
    patch_count = NX // (PR * lax.axis_size("dev"))
    leading_patch = lax.axis_index("dev") * patch_count
    patch_index = leading_patch + jnp.arange(patch_count, dtype=jnp.int32)
    nearby_readers = lax.dynamic_slice_in_dim(readers, leading_patch, patch_count, 0)
    local_counts = lax.dynamic_slice_in_dim(counts, leading_patch, patch_count, 0)
    weights = obs_weights(patch_index, nearby_readers, local_counts, obs_block, obs_var)
    for cycle in range(CYCLES):
        finished = []
        pieces = []
        for variable in range(V):
            advanced_fields = prior_guess(
                sample_ensemble[:, variable], flow_speed, spreading_coefficient[variable]
            )
            finished.append(advanced_fields)
            pieces.append(
                lax.all_to_all(advanced_fields, "dev", split_axis=1, concat_axis=0, tiled=True)
            )
        sample_ensemble = jnp.stack(finished, 1)
        patches = jnp.stack(pieces, 1)
        model_obs = jnp.take(block_means(sample_ensemble), obs_block, axis=1)
        all_obs = lax.all_gather(model_obs, "dev", axis=0, tiled=True)
        obs_rows = jnp.take(all_obs, nearby_readers, axis=1)
        sensor_readings = obs_values[cycle][nearby_readers]
        updated = analyse(patches, obs_rows, sensor_readings, weights)
        sample_ensemble = lax.all_to_all(updated, "dev", split_axis=0, concat_axis=2, tiled=True)
    return sample_ensemble


def solution(mesh):
    return jax.shard_map(
        local,
        mesh=mesh,
        in_specs=(P("dev", None, None, None), P(), P(), P(), P(), P(), P(), P()),
        out_specs=P("dev", None, None, None),
        check_vma=False,
    )
```

profile of v0, /device:TPU:0, one launch (start us, length us, event | category | flops | bytes accessed | tf_op | source)
XLA Modules:
  0.0 1134.6 jit_solution(4595288333743894645)
XLA Ops:
  11.9 2.8 slice_bitcast_fusion.481
  14.8 3.8 slice_bitcast_fusion.479
  70.3 7.9 all-to-all-start.3
  81.8 2.7 subtract_add_fusion.17
  229.6 19.4 %multiply_add_fusion.28 = f32[4,1,256,256]{3,2,0,1:T(8,128)} fusion(f32[4,1,256,255]{3,2,0,1:T(8,128)} %get-tuple-element.1278, f32[4,1,256,1]{3,2,0,1:T(8,128)} %get-tuple-element.1282, f32[4,1,256,1]{3,2,0,1:T(8,128)} %get-tuple-element.1281, f32[4,1,256,255]{3,2,0,1:T(8,128)} %get-tuple-element.1277, f32[4,1,255,256]{3,2,0,1:T(8,128)} %get-tuple-element.1270, ...), kind=kLoop, calls=%fused_computation.740 | loop fusion | flops 47185920 | bytes 40632320 | tf_op jit(solution)/shard_map/add | solution.py:42
  249.2 18.5 %multiply_add_fusion.29 = f32[4,1,256,256]{3,2,0,1:T(8,128)} fusion(f32[4,1,256,255]{3,2,0,1:T(8,128)} %get-tuple-element.1134, f32[4,1,256,1]{3,2,0,1:T(8,128)} %get-tuple-element.1138, f32[4,1,256,1]{3,2,0,1:T(8,128)} %get-tuple-element.1137, f32[4,1,256,255]{3,2,0,1:T(8,128)} %get-tuple-element.1133, f32[4,1,255,256]{3,2,0,1:T(8,128)} %get-tuple-element.1126, ...), kind=kLoop, calls=%fused_computation.741 | loop fusion | flops 47185920 | bytes 40632320 | tf_op jit(solution)/shard_map/add | solution.py:42
  271.2 17.5 %multiply_add_fusion.30 = f32[4,1,256,256]{3,2,0,1:T(8,128)} fusion(f32[4,1,256,255]{3,2,0,1:T(8,128)} %get-tuple-element.990, f32[4,1,256,1]{3,2,0,1:T(8,128)} %get-tuple-element.994, f32[4,1,256,1]{3,2,0,1:T(8,128)} %get-tuple-element.993, f32[4,1,256,255]{3,2,0,1:T(8,128)} %get-tuple-element.989, f32[4,1,255,256]{3,2,0,1:T(8,128)} %get-tuple-element.982, ...), kind=kLoop, calls=%fused_computation.742 | loop fusion | flops 47185920 | bytes 40632320 | tf_op jit(solution)/shard_map/add | solution.py:42
  288.7 6.3 all-to-all-start.2
  295.1 19.2 %multiply_add_fusion.31 = f32[4,1,256,256]{3,2,0,1:T(8,128)S(1)} fusion(f32[4,1,256,255]{3,2,0,1:T(8,128)} %get-tuple-element.846, f32[4,1,256,1]{3,2,0,1:T(8,128)} %get-tuple-element.850, f32[4,1,256,1]{3,2,0,1:T(8,128)} %get-tuple-element.849, f32[4,1,256,255]{3,2,0,1:T(8,128)} %get-tuple-element.845, f32[4,1,255,256]{3,2,0,1:T(8,128)} %get-tuple-element.838, ...), kind=kLoop, calls=%fused_computation.743 | loop fusion | flops 47185920 | bytes 40632320 | tf_op jit(solution)/shard_map/add | solution.py:42
  323.4 4.9 copy.4452
  328.3 17.6 %gather_fusion.4 = f32[4096,4]{1,0:T(8,128)} fusion(f32[4,16384]{0,1:T(8,128)} %bitcast.1699, s32[4096]{0:T(1024)S(1)} %fusion.100), kind=kCustom, calls=%fused_computation.clone | custom fusion | bytes 147456 | tf_op jit(solution)/shard_map/jit(_take)/gather | solution.py:135
  345.9 6.1 all-to-all-start.1
  352.0 4.7 select_bitcast_fusion.1
  356.7 2.8 copy.4249
  359.6 3.5 multiply_add_fusion.50
  364.8 14.3 %all-to-all-done.1 = f32[4,256,256]{2,0,1:T(4,128)} async-done(((f32[4,256,256]{2,0,1:T(4,128)}), f32[4,256,256]{2,0,1:T(4,128)}, u32[]{:S(2)}, u32[]{:S(2)}) %all-to-all-start.1) | async-done | bytes 1048608 | tf_op jit(solution)/shard_map/all_to_all | solution.py:131
  379.2 3.8 all-to-all-start
  383.8 3.1 gather_fusion
  386.9 3.1 gather_fusion.1
  390.7 3.1 gather_fusion.2
  415.9 2.7 stack.60
  429.1 2.9 reshape.16550
  432.0 3.0 copy.4250
  435.0 2.6 gather_fusion.5
  439.5 17.7 %while.26 = (s32[]{:T(128)}, f32[4,128,128]{1,2,0:T(8,128)S(1)}, f32[4,128,128]{2,1,0:T(8,128)S(1)}, s32[]{:T(128)}) while((s32[]{:T(128)}, f32[4,128,128]{1,2,0:T(8,128)S(1)}, f32[4,128,128]{2,1,0:T(8,128)S(1)}, s32[]{:T(128)}) %tuple.969), condition=%wide.region_5.8_spmd.clone, body=%wide.region_4.7_spmd.clone.sunk | while | flops 302153728 | bytes 3538997 | solution.py:98
  458.3 6.0 bitcast_add_fusion.1
  467.2 97.0 %all_to_all.156 = f32[128,4,8,256]{3,2,1,0:T(8,128)S(1)} all-to-all(f32[128,4,8,256]{3,2,1,0:T(8,128)S(1)} %copy.4255), channel_id=1, replica_groups=mesh['dev'=32] {'dev'}, dimensions={0} | all-to-all | bytes 8388608 | tf_op jit(solution)/shard_map/all_to_all | solution.py:140
  777.0 16.5 %multiply_add_fusion = f32[4,1,256,256]{3,2,0,1:T(8,128)S(1)} fusion(f32[4,1,256,255]{3,2,0,1:T(8,128)} %get-tuple-element.702, f32[4,1,256,1]{3,2,0,1:T(8,128)} %get-tuple-element.706, f32[4,1,256,1]{3,2,0,1:T(8,128)} %get-tuple-element.705, f32[4,1,256,255]{3,2,0,1:T(8,128)} %get-tuple-element.701, f32[4,1,255,256]{3,2,0,1:T(8,128)} %get-tuple-element.694, ...), kind=kLoop, calls=%fused_computation.700 | loop fusion | flops 47185920 | bytes 40632320 | tf_op jit(solution)/shard_map/add | solution.py:42
  795.2 4.2 all-to-all-start.8
  799.6 3.8 multiply_add_fusion.22
  806.0 18.5 %multiply_add_fusion.3 = f32[4,1,256,256]{3,2,0,1:T(8,128)S(1)} fusion(f32[4,1,256,255]{3,2,0,1:T(8,128)} %get-tuple-element.270, f32[4,1,256,1]{3,2,0,1:T(8,128)} %get-tuple-element.274, f32[4,1,256,1]{3,2,0,1:T(8,128)} %get-tuple-element.273, f32[4,1,256,255]{3,2,0,1:T(8,128)} %get-tuple-element.269, f32[4,1,255,256]{3,2,0,1:T(8,128)} %get-tuple-element.262, ...), kind=kLoop, calls=%fused_computation.703 | loop fusion | flops 47185920 | bytes 40632320 | tf_op jit(solution)/shard_map/add | solution.py:42
  830.9 16.3 %multiply_add_fusion.2 = f32[4,1,256,256]{3,2,0,1:T(8,128)S(1)} fusion(f32[4,1,256,255]{3,2,0,1:T(8,128)} %get-tuple-element.414, f32[4,1,256,1]{3,2,0,1:T(8,128)} %get-tuple-element.418, f32[4,1,256,1]{3,2,0,1:T(8,128)} %get-tuple-element.417, f32[4,1,256,255]{3,2,0,1:T(8,128)} %get-tuple-element.413, f32[4,1,255,256]{3,2,0,1:T(8,128)} %get-tuple-element.406, ...), kind=kLoop, calls=%fused_computation.702 | loop fusion | flops 47185920 | bytes 40632320 | tf_op jit(solution)/shard_map/add | solution.py:42
  859.0 6.1 all-to-all-start.5
  865.2 19.1 %multiply_add_fusion.1 = f32[4,1,256,256]{3,2,0,1:T(8,128)S(1)} fusion(f32[4,1,256,255]{3,2,0,1:T(8,128)} %get-tuple-element.558, f32[4,1,256,1]{3,2,0,1:T(8,128)} %get-tuple-element.562, f32[4,1,256,1]{3,2,0,1:T(8,128)} %get-tuple-element.561, f32[4,1,256,255]{3,2,0,1:T(8,128)} %get-tuple-element.557, f32[4,1,255,256]{3,2,0,1:T(8,128)} %get-tuple-element.550, ...), kind=kLoop, calls=%fused_computation.701 | loop fusion | flops 47185920 | bytes 40632320 | tf_op jit(solution)/shard_map/add | solution.py:42
  888.6 6.1 copy.4456
  894.7 17.6 %gather_fusion.6 = f32[4096,4]{1,0:T(8,128)} fusion(f32[4,16384]{0,1:T(8,128)} %bitcast.1700, s32[4096]{0:T(1024)S(1)} %copy-done.134), kind=kCustom, calls=%fused_computation.2.clone | custom fusion | bytes 147456 | tf_op jit(solution)/shard_map/jit(_take)/gather | solution.py:135
  912.3 5.9 all-to-all-start.6
  918.2 4.9 select_bitcast_fusion
  923.2 2.8 copy.4423
  926.0 3.4 multiply_add_fusion.10
  931.1 14.3 %all-to-all-done.6 = f32[4,256,256]{2,0,1:T(4,128)} async-done(((f32[4,256,256]{2,0,1:T(4,128)}), f32[4,256,256]{2,0,1:T(4,128)}, u32[]{:S(2)}, u32[]{:S(2)}) %all-to-all-start.6) | async-done | bytes 1048608 | tf_op jit(solution)/shard_map/all_to_all | solution.py:131
  945.3 3.6 all-to-all-start.7
  949.0 3.1 gather_fusion.3
  968.1 12.0 %all-to-all-done.7 = f32[4,256,256]{2,0,1:T(4,128)S(1)} async-done(((f32[4,256,256]{2,0,1:T(4,128)}), f32[4,256,256]{2,0,1:T(4,128)S(1)}, u32[]{:S(2)}, u32[]{:S(2)}) %all-to-all-start.7) | async-done | bytes 1048608 | tf_op jit(solution)/shard_map/all_to_all | solution.py:131
  992.7 2.9 reshape.16552
  1000.4 17.6 %while.27 = (s32[]{:T(128)}, f32[4,128,128]{1,2,0:T(8,128)S(1)}, f32[4,128,128]{2,1,0:T(8,128)S(1)}, s32[]{:T(128)}) while((s32[]{:T(128)}, f32[4,128,128]{1,2,0:T(8,128)S(1)}, f32[4,128,128]{2,1,0:T(8,128)S(1)}, s32[]{:T(128)}) %tuple.972), condition=%wide.region_11.14_spmd.clone, body=%wide.region_10.13_spmd.clone.sunk | while | flops 302153728 | bytes 3538997 | solution.py:98
  1019.1 5.8 bitcast_add_fusion
  1027.9 96.9 %all_to_all.157 = f32[128,4,8,256]{3,2,1,0:T(8,128)S(1)} all-to-all(f32[128,4,8,256]{3,2,1,0:T(8,128)S(1)} %copy.4429), channel_id=1, replica_groups=mesh['dev'=32] {'dev'}, dimensions={0} | all-to-all | bytes 8388608 | tf_op jit(solution)/shard_map/all_to_all | solution.py:140
  (1003 shorter events, 572.6 us)
Async XLA Ops:
  6.5 380.4 %copy-start = (f32[4096]{0:T(1024)S(1)}, f32[4096]{0:T(1024)}, u32[]{:S(2)}) copy-start(f32[4096]{0:T(1024)} %param.20) | copy-start | bytes 49156
  18.8 49.0 %copy-start.10 = (f32[256,256]{1,0:T(8,128)}, f32[256,256]{1,0:T(8,128)S(1)}, u32[]{:S(2)}) copy-start(f32[256,256]{1,0:T(8,128)S(1)} %get-tuple-element.1285) | copy-start | bytes 786436
  18.8 230.3 %copy-start.6 = (f32[256,256]{1,0:T(8,128)}, f32[256,256]{1,0:T(8,128)S(1)}, u32[]{:S(2)}) copy-start(f32[256,256]{1,0:T(8,128)S(1)} %get-tuple-element.1288) | copy-start | bytes 786436
  18.8 297.0 %copy-start.8 = (f32[256,256]{1,0:T(8,128)}, f32[256,256]{1,0:T(8,128)S(1)}, u32[]{:S(2)}) copy-start(f32[256,256]{1,0:T(8,128)S(1)} %get-tuple-element.1286) | copy-start | bytes 786436
  70.3 218.3 %all-to-all-start.3 = ((f32[4,256,256]{2,0,1:T(4,128)}), f32[4,256,256]{2,0,1:T(4,128)}, u32[]{:S(2)}, u32[]{:S(2)}) async-start(f32[4,256,256]{2,0,1:T(4,128)} %copy.4096), calls=%async_computation.3 | async-start | bytes 2097152 | tf_op jit(solution)/shard_map/all_to_all | solution.py:131
  221.8 47.7 %copy-start.28 = (f32[4,256,256]{2,1,0:T(8,128)}, f32[4,256,256]{2,1,0:T(8,128)S(1)}, u32[]{:S(2)}) copy-start(f32[4,256,256]{2,1,0:T(8,128)S(1)} %multiply_add_fusion.51) | copy-start | bytes 3145732
  249.1 21.9 %copy-start.116 = (f32[4,1,255,256]{3,2,0,1:T(8,128)S(1)}, f32[4,1,255,256]{3,2,0,1:T(8,128)}, u32[]{:S(2)}) copy-start(f32[4,1,255,256]{3,2,0,1:T(8,128)} %get-tuple-element.886) | copy-start | bytes 3133444
  249.1 21.9 %copy-start.117 = (f32[4,1,256,255]{3,2,0,1:T(8,128)S(1)}, f32[4,1,256,255]{3,2,0,1:T(8,128)}, u32[]{:S(2)}) copy-start(f32[4,1,256,255]{3,2,0,1:T(8,128)} %get-tuple-element.893) | copy-start | bytes 3133444
  249.2 21.9 %copy-start.118 = (f32[4,1,256,255]{3,2,0,1:T(8,128)S(1)}, f32[4,1,256,255]{3,2,0,1:T(8,128)}, u32[]{:S(2)}) copy-start(f32[4,1,256,255]{3,2,0,1:T(8,128)} %get-tuple-element.894) | copy-start | bytes 3133444
  249.2 21.9 %copy-start.119 = (f32[4,1,255,256]{3,2,0,1:T(8,128)S(1)}, f32[4,1,255,256]{3,2,0,1:T(8,128)}, u32[]{:S(2)}) copy-start(f32[4,1,255,256]{3,2,0,1:T(8,128)} %get-tuple-element.901) | copy-start | bytes 3133444
  271.2 23.8 %copy-start.150 = (f32[4,1,1,256]{3,2,0,1:T(1,128)S(1)}, f32[4,1,1,256]{3,2,0,1:T(1,128)}, u32[]{:S(2)}) copy-start(f32[4,1,1,256]{3,2,0,1:T(1,128)} %get-tuple-element.1310) | copy-start | bytes 12292
  271.2 23.8 %copy-start.151 = (f32[4,1,1,256]{3,2,0,1:T(1,128)S(1)}, f32[4,1,1,256]{3,2,0,1:T(1,128)}, u32[]{:S(2)}) copy-start(f32[4,1,1,256]{3,2,0,1:T(1,128)} %get-tuple-element.1311) | copy-start | bytes 12292
  271.2 23.8 %copy-start.195 = (f32[4,1,1,256]{3,2,0,1:T(1,128)S(1)}, f32[4,1,1,256]{3,2,0,1:T(1,128)}, u32[]{:S(2)}) copy-start(f32[4,1,1,256]{3,2,0,1:T(1,128)} %get-tuple-element.729) | copy-start | bytes 12292
  271.2 23.8 %copy-start.196 = (f32[4,1,1,256]{3,2,0,1:T(1,128)S(1)}, f32[4,1,1,256]{3,2,0,1:T(1,128)}, u32[]{:S(2)}) copy-start(f32[4,1,1,256]{3,2,0,1:T(1,128)} %get-tuple-element.730) | copy-start | bytes 12292
  288.7 57.2 %all-to-all-start.2 = ((f32[4,256,256]{2,0,1:T(4,128)}), f32[4,256,256]{2,0,1:T(4,128)}, u32[]{:S(2)}, u32[]{:S(2)}) async-start(f32[4,256,256]{2,0,1:T(4,128)} %copy.4092), calls=%async_computation.2 | async-start | bytes 2097152 | tf_op jit(solution)/shard_map/all_to_all | solution.py:131
  295.0 20.0 %copy-start.64 = (f32[4,1,256,256]{3,2,0,1:T(8,128)S(1)}, f32[4,1,256,256]{3,2,0,1:T(8,128)}, u32[]{:S(2)}) copy-start(f32[4,1,256,256]{3,2,0,1:T(8,128)} %multiply_add_fusion.29) | copy-start | bytes 3145732
  295.0 20.7 %copy-start.48 = (f32[4,256,255]{2,1,0:T(8,128)S(1)}, f32[4,256,255]{2,1,0:T(8,128)}, u32[]{:S(2)}) copy-start(f32[4,256,255]{2,1,0:T(8,128)} %get-tuple-element.992) | copy-start | bytes 3133444
  295.1 20.7 %copy-start.124 = (f32[4,256,1]{2,1,0:T(8,128)S(1)}, f32[4,256,1]{2,1,0:T(8,128)}, u32[]{:S(2)}) copy-start(f32[4,256,1]{2,1,0:T(8,128)} %get-tuple-element.996) | copy-start | bytes 12292
  328.3 31.3 %copy-start.133 = (s32[4096]{0:T(1024)}, s32[4096]{0:T(1024)S(1)}, u32[]{:S(2)}) copy-start(s32[4096]{0:T(1024)S(1)} %fusion.100) | copy-start | bytes 49156
  345.9 33.3 %all-to-all-start.1 = ((f32[4,256,256]{2,0,1:T(4,128)}), f32[4,256,256]{2,0,1:T(4,128)}, u32[]{:S(2)}, u32[]{:S(2)}) async-start(f32[4,256,256]{2,0,1:T(4,128)} %copy.4088), calls=%async_computation.1 | async-start | bytes 2097152 | tf_op jit(solution)/shard_map/all_to_all | solution.py:131
  352.0 77.1 %all-gather.5.cloned.1.call-start = ((), (), s32[]{:S(2)}) async-start(), calls=%async_computation.10 | async-start | bytes 2162688 | tf_op jit(solution)/shard_map/all_gather | solution.py:136
  363.2 19.8 %copy-start.211 = (s32[128]{0:T(128)S(1)}, s32[128]{0:T(128)}, u32[]{:S(2)}) copy-start(s32[128]{0:T(128)} %param.23) | copy-start | bytes 1540
  363.2 26.9 %copy-start.143 = (f32[2,4096]{1,0:T(2,128)S(1)}, f32[2,4096]{1,0:T(2,128)}, u32[]{:S(2)}) copy-start(f32[2,4096]{1,0:T(2,128)} %param.19) | copy-start | bytes 98308
  379.2 34.9 %all-to-all-start = ((f32[4,256,256]{2,0,1:T(4,128)}), f32[4,256,256]{2,0,1:T(4,128)S(1)}, u32[]{:S(2)}, u32[]{:S(2)}) async-start(f32[4,256,256]{2,0,1:T(4,128)} %copy.4084), calls=%async_computation | async-start | bytes 2097152 | tf_op jit(solution)/shard_map/all_to_all | solution.py:131
  383.0 56.5 %copy-start.129 = (f32[128,128]{1,0:T(8,128)}, f32[128,128]{1,0:T(8,128)S(1)}, u32[]{:S(2)}) copy-start(f32[128,128]{1,0:T(8,128)S(1)} %fusion.94) | copy-start | bytes 196612
  383.8 51.2 %copy-start.135 = (s32[1024]{0:T(1024)}, s32[1024]{0:T(1024)S(1)}, u32[]{:S(2)}) copy-start(s32[1024]{0:T(1024)S(1)} %pad_clamp_fusion) | copy-start | bytes 12292
  394.6 43.8 %copy-start.137 = (pred[4,128]{1,0:T(4,128)(4,1)}, pred[4,128]{1,0:T(4,128)(4,1)S(1)}, u32[]{:S(2)}) copy-start(pred[4,128]{1,0:T(4,128)(4,1)S(1)} %compare_and_fusion.1) | copy-start | bytes 1540
  564.6 210.4 %copy-start.4 = (f32[4,4,32,8,256]{4,3,2,1,0:T(8,128)}, f32[4,4,32,8,256]{4,3,2,1,0:T(8,128)S(1)}, u32[]{:S(2)}) copy-start(f32[4,4,32,8,256]{4,3,2,1,0:T(8,128)S(1)} %copy.4482) | copy-start | bytes 12582916
  795.2 63.8 %all-to-all-start.8 = ((f32[4,256,256]{2,0,1:T(4,128)}), f32[4,256,256]{2,0,1:T(4,128)}, u32[]{:S(2)}, u32[]{:S(2)}) async-start(f32[4,256,256]{2,0,1:T(4,128)} %copy.4270), calls=%async_computation.8 | async-start | bytes 2097152 | tf_op jit(solution)/shard_map/all_to_all | solution.py:131
  805.9 20.2 %copy-start.20 = (f32[4,256,256]{2,1,0:T(8,128)S(1)}, f32[4,256,256]{2,1,0:T(8,128)}, u32[]{:S(2)}) copy-start(f32[4,256,256]{2,1,0:T(8,128)} %copy-done.19) | copy-start | bytes 3145732
  805.9 20.2 %copy-start.30 = (f32[4,256,256]{2,1,0:T(8,128)S(1)}, f32[4,256,256]{2,1,0:T(8,128)}, u32[]{:S(2)}) copy-start(f32[4,256,256]{2,1,0:T(8,128)} %copy-done.29) | copy-start | bytes 3145732
  805.9 20.2 %copy-start.49 = (f32[4,255,256]{2,1,0:T(8,128)S(1)}, f32[4,255,256]{2,1,0:T(8,128)}, u32[]{:S(2)}) copy-start(f32[4,255,256]{2,1,0:T(8,128)} %get-tuple-element.407) | copy-start | bytes 3133444
  805.9 20.2 %copy-start.50 = (f32[4,255,256]{2,1,0:T(8,128)S(1)}, f32[4,255,256]{2,1,0:T(8,128)}, u32[]{:S(2)}) copy-start(f32[4,255,256]{2,1,0:T(8,128)} %get-tuple-element.408) | copy-start | bytes 3133444
  805.9 20.2 %copy-start.51 = (f32[4,256,255]{2,1,0:T(8,128)S(1)}, f32[4,256,255]{2,1,0:T(8,128)}, u32[]{:S(2)}) copy-start(f32[4,256,255]{2,1,0:T(8,128)} %get-tuple-element.415) | copy-start | bytes 3133444
  805.9 20.2 %copy-start.52 = (f32[4,256,255]{2,1,0:T(8,128)S(1)}, f32[4,256,255]{2,1,0:T(8,128)}, u32[]{:S(2)}) copy-start(f32[4,256,255]{2,1,0:T(8,128)} %get-tuple-element.416) | copy-start | bytes 3133444
  806.0 24.3 %copy-start.112 = (f32[4,1,255,256]{3,2,0,1:T(8,128)S(1)}, f32[4,1,255,256]{3,2,0,1:T(8,128)}, u32[]{:S(2)}) copy-start(f32[4,1,255,256]{3,2,0,1:T(8,128)} %get-tuple-element.325) | copy-start | bytes 3133444
  806.0 24.3 %copy-start.113 = (f32[4,1,255,256]{3,2,0,1:T(8,128)S(1)}, f32[4,1,255,256]{3,2,0,1:T(8,128)}, u32[]{:S(2)}) copy-start(f32[4,1,255,256]{3,2,0,1:T(8,128)} %get-tuple-element.326) | copy-start | bytes 3133444
  806.0 24.3 %copy-start.114 = (f32[4,1,256,255]{3,2,0,1:T(8,128)S(1)}, f32[4,1,256,255]{3,2,0,1:T(8,128)}, u32[]{:S(2)}) copy-start(f32[4,1,256,255]{3,2,0,1:T(8,128)} %get-tuple-element.333) | copy-start | bytes 3133444
  859.0 53.3 %all-to-all-start.5 = ((f32[4,256,256]{2,0,1:T(4,128)}), f32[4,256,256]{2,0,1:T(4,128)}, u32[]{:S(2)}, u32[]{:S(2)}) async-start(f32[4,256,256]{2,0,1:T(4,128)} %copy.4258), calls=%async_computation.5 | async-start | bytes 2097152 | tf_op jit(solution)/shard_map/all_to_all | solution.py:131
  865.2 19.8 %copy-start.35 = (f32[4,1,256,256]{3,0,2,1:T(4,128)S(1)}, f32[4,1,256,256]{3,0,2,1:T(4,128)}, u32[]{:S(2)}) copy-start(f32[4,1,256,256]{3,0,2,1:T(4,128)} %copy.4455) | copy-start | bytes 3145732
  865.2 19.8 %copy-start.36 = (f32[4,1,256,256]{3,0,2,1:T(4,128)S(1)}, f32[4,1,256,256]{3,0,2,1:T(4,128)}, u32[]{:S(2)}) copy-start(f32[4,1,256,256]{3,0,2,1:T(4,128)} %copy.4309) | copy-start | bytes 3145732
  865.2 19.8 %copy-start.37 = (f32[4,1,256,256]{3,0,2,1:T(4,128)S(1)}, f32[4,1,256,256]{3,0,2,1:T(4,128)}, u32[]{:S(2)}) copy-start(f32[4,1,256,256]{3,0,2,1:T(4,128)} %copy.4346) | copy-start | bytes 3145732
  888.6 29.6 %copy-start.140 = (pred[4096]{0:T(1024)(128)(4,1)S(1)}, pred[4096]{0:T(1024)(128)(4,1)}, u32[]{:S(2)}) copy-start(pred[4096]{0:T(1024)(128)(4,1)} %copy-done.139) | copy-start | bytes 12292
  912.3 33.1 %all-to-all-start.6 = ((f32[4,256,256]{2,0,1:T(4,128)}), f32[4,256,256]{2,0,1:T(4,128)}, u32[]{:S(2)}, u32[]{:S(2)}) async-start(f32[4,256,256]{2,0,1:T(4,128)} %copy.4262), calls=%async_computation.6 | async-start | bytes 2097152 | tf_op jit(solution)/shard_map/all_to_all | solution.py:131
  918.2 74.5 %all-gather.7.cloned.1.call-start = ((), (), s32[]{:S(2)}) async-start(), calls=%async_computation.11 | async-start | bytes 2162688 | tf_op jit(solution)/shard_map/all_gather | solution.py:136
  929.4 19.6 %copy-start.3 = (f32[1,4096]{1,0:T(1,128)S(1)}, f32[1,4096]{1,0:T(1,128)}, u32[]{:S(2)}) copy-start(f32[1,4096]{1,0:T(1,128)} %get-tuple-element.1291) | copy-start | bytes 49156
  929.4 19.6 %copy-start.136 = (s32[1024]{0:T(1024)S(1)}, s32[1024]{0:T(1024)}, u32[]{:S(2)}) copy-start(s32[1024]{0:T(1024)} %copy-done.135) | copy-start | bytes 12292
  945.3 34.8 %all-to-all-start.7 = ((f32[4,256,256]{2,0,1:T(4,128)}), f32[4,256,256]{2,0,1:T(4,128)S(1)}, u32[]{:S(2)}, u32[]{:S(2)}) async-start(f32[4,256,256]{2,0,1:T(4,128)} %copy.4266), calls=%async_computation.7 | async-start | bytes 2097152 | tf_op jit(solution)/shard_map/all_to_all | solution.py:131
  (174 other events, 1005.2 us)
Sparse Core Ops, SparseCore 0:
  359.7 63.1 all-gather.4
  926.1 62.7 all-gather.6
where the time goes:
time: 1150 us; the launch traced here: 1130 us
  local copies, waits for them, and re-layouts  539 us (47%)
  other arithmetic  244 us (21%)
  blocking collectives  194 us (17%)
  matrix products  51.8 us (5%)
  starting transfers between devices  43.9 us (4%)
  waiting for transfers between devices  43.3 us (4%)
  between operations  17.5 us (2%)
    concatenate x140, local copies, waits for them, and re-layouts, tendency(): shifted_left = jnp.roll(sample_ensemble, -1, axis=-1)  218 us
    all_to_all x2, blocking collectives, local(): lax.all_to_all(updated, 'dev', split_axis=0, concat_axis=2, tiled=True)  194 us
    add x32, other arithmetic, prior_guess(): sample_ensemble / 3.0  178 us
    concatenate x140, local copies, waits for them, and re-layouts, tendency(): shifted_up = jnp.roll(sample_ensemble, -1, axis=-2)  142 us
    all_to_all x8, starting transfers between devices, local(): lax.all_to_all(advanced_fields, 'dev', split_axis=1, concat_axis=0, tiled...  43.8 us
    all_to_all x8, waiting for transfers between devices, local(): lax.all_to_all(advanced_fields, 'dev', split_axis=1, concat_axis=0, tiled...  43.2 us
    unnamed x438, local copies, waits for them, and re-layouts  38 us
    gather x2, local copies, waits for them, and re-layouts, local(): model_obs = jnp.take(block_means(sample_ensemble), obs_block, axis=1)  35.1 us
  transfers between devices with their start and end apart: 10, of which 4 were waited for; matrix products, arithmetic and copies ran while one was open for 41% of the time, Pallas kernels for 0%

commit v1 on v0

v1 whole, which is shorter than its diff:
```python
import functools

import jax
import jax.numpy as jnp
from jax import lax
from jax.experimental import pallas as pl
from jax.experimental.pallas import tpu as pltpu
from jax.sharding import PartitionSpec as P

PR = 2
BLOCK = 4
STEPS = 3
CYCLES = 2
NS_ITERS = 10
TAPER_ROWS = 6.0
HALO = 3 * STEPS
SUB = 8
MT = 16
F32 = jnp.float32
BF16 = jnp.bfloat16


def exact_dot(a, b):
    return jnp.dot(a, b, precision=lax.Precision.HIGHEST, preferred_element_type=F32)


def halves(x):
    hi = x.astype(BF16)
    return hi, (x - hi.astype(F32)).astype(BF16)


def thirds(x):
    hi = x.astype(BF16)
    rest = x - hi.astype(F32)
    mid = rest.astype(BF16)
    return hi, mid, (rest - mid.astype(F32)).astype(BF16)


def bdot(a, b):
    return jnp.dot(a, b, preferred_element_type=F32)


def dot3(a, b):
    (ah, al), (bh, bl) = a, b
    return bdot(ah, bh) + (bdot(ah, bl) + bdot(al, bh))


def member_forecast_kernel(
    owner_rows, q_ref, flow_ref, spread_ref, col_ref, var_ref, out_ref, hx_ref, coef, buf_q, buf_a, buf_b
):
    v = pl.program_id(0)
    nx, ny = buf_q.shape
    strips = nx // SUB
    sub = lax.broadcasted_iota(jnp.int32, (SUB, ny), 0)

    def rows(i):
        return pl.ds(pl.multiple_of(i * SUB, SUB), SUB)

    def fill(i, _):
        s = rows(i)
        sc = spread_ref[0, s, :]
        fx = 0.5 * flow_ref[0, s, :]
        fy = 0.5 * flow_ref[1, s, :]
        coef[0, s, :] = 1.0 - 4.0 * sc
        coef[1, s, :] = sc - fx
        coef[2, s, :] = sc + fx
        coef[3, s, :] = sc - fy
        coef[4, s, :] = sc + fy
        return 0

    lax.fori_loop(0, strips, fill, 0, unroll=2)

    def stage(src, write):
        def body(i, carry):
            cur, cur_up, prev_dn = carry
            nxt = src(lax.rem(i + 1, strips))
            nxt_up = pltpu.roll(nxt, SUB - 1, 0)
            cur_dn = pltpu.roll(cur, 1, 0)
            up = jnp.where(sub == SUB - 1, nxt_up, cur_up)
            dn = jnp.where(sub == 0, prev_dn, cur_dn)
            left = pltpu.roll(cur, ny - 1, 1)
            right = pltpu.roll(cur, 1, 1)
            s = rows(i)
            t = (
                coef[0, s, :] * cur
                + (coef[1, s, :] * up + coef[2, s, :] * dn)
                + (coef[3, s, :] * left + coef[4, s, :] * right)
            )
            write(s, t)
            return nxt, nxt_up, cur_dn

        first = src(0)
        lax.fori_loop(
            0,
            strips,
            body,
            (first, pltpu.roll(first, SUB - 1, 0), pltpu.roll(src(strips - 1), 1, 0)),
            unroll=4,
        )

    for step in range(STEPS):
        if step == 0:
            base = lambda s: q_ref[0, 0, s, :]
        else:
            base = lambda s: buf_q[s, :]

        def write_a(s, t):
            buf_a[s, :] = t

        def write_b(s, t, base=base):
            buf_b[s, :] = 0.75 * base(s) + 0.25 * t

        def write_q(s, t, base=base):
            buf_q[s, :] = base(s) * (1.0 / 3.0) + (2.0 / 3.0) * t

        stage(lambda i, base=base: base(rows(i)), write_a)
        stage(lambda i: buf_a[rows(i), :], write_b)
        stage(lambda i: buf_b[rows(i), :], write_q)

    height = out_ref.shape[2]
    for g, r in enumerate(owner_rows):
        out_ref[g, 0] = buf_q[r * height : (r + 1) * height, :]

    nbr, nbc = nx // BLOCK, ny // BLOCK
    lanes = hx_ref.shape[1]
    pool_rows = (
        lax.broadcasted_iota(jnp.int32, (nbr, nx), 1) // BLOCK
        == lax.broadcasted_iota(jnp.int32, (nbr, nx), 0)
    ).astype(F32)
    pool_cols = (
        lax.broadcasted_iota(jnp.int32, (ny, lanes), 0) // BLOCK
        == lax.broadcasted_iota(jnp.int32, (ny, lanes), 1)
    ).astype(F32)
    pooled = exact_dot(exact_dot(pool_rows, buf_q[...]), pool_cols) * (1.0 / (BLOCK * BLOCK))
    chosen = jnp.take_along_axis(pooled, col_ref[...], axis=1, mode="promise_in_bounds")
    chosen = jnp.where(var_ref[...] == v, chosen, 0.0)

    @pl.when(v == 0)
    def _():
        hx_ref[...] = chosen

    @pl.when(v > 0)
    def _():
        hx_ref[...] += chosen


def member_forecast(j, ensemble, flow, spread, col, var, owner_rows):
    _, nv, nx, ny = ensemble.shape
    groups = len(owner_rows)
    height = nx // groups
    return pl.pallas_call(
        functools.partial(member_forecast_kernel, owner_rows),
        grid=(nv,),
        in_specs=[
            pl.BlockSpec((1, 1, nx, ny), lambda v: (j, v, 0, 0)),
            pl.BlockSpec((2, nx, ny), lambda v: (0, 0, 0)),
            pl.BlockSpec((1, nx, ny), lambda v: (v, 0, 0)),
            pl.BlockSpec(col.shape, lambda v: (0, 0)),
            pl.BlockSpec(var.shape, lambda v: (0, 0)),
        ],
        out_specs=[
            pl.BlockSpec((groups, 1, height, ny), lambda v: (0, v, 0, 0)),
            pl.BlockSpec(col.shape, lambda v: (0, 0)),
        ],
        out_shape=[
            jax.ShapeDtypeStruct((groups, nv, height, ny), F32),
            jax.ShapeDtypeStruct(col.shape, F32),
        ],
        scratch_shapes=[pltpu.VMEM((5, nx, ny), F32)] + [pltpu.VMEM((nx, ny), F32)] * 3,
        name="member_forecast",
    )(ensemble, flow, spread, col, var)


def transform_kernel(base_ref, hx_ref, chosen_ref, weight_ref, value_ref, out_ref):
    blocks, members, width = hx_ref.shape
    count, _, slots = chosen_ref.shape
    chosen = jnp.concatenate([chosen_ref[p] for p in range(count)], axis=1)
    row = lax.broadcasted_iota(jnp.int32, (width, count * slots), 0)

    def gather(b, acc):
        pick = (row + base_ref[b] == chosen).astype(F32).astype(BF16)
        hi, mid, lo = thirds(hx_ref[b])
        return acc + (bdot(hi, pick) + (bdot(mid, pick) + bdot(lo, pick)))

    hx = lax.fori_loop(0, blocks, gather, jnp.zeros((members, count * slots), F32))
    eye = (
        lax.broadcasted_iota(jnp.int32, (members, members), 0)
        == lax.broadcasted_iota(jnp.int32, (members, members), 1)
    ).astype(F32)
    scale = 1.0 / (members - 1)
    roots, drives, norms = [], [], []
    for p in range(count):
        part = hx[:, p * slots : (p + 1) * slots]
        mean = jnp.mean(part, axis=0, keepdims=True)
        y = part - mean
        w = weight_ref[p]
        gram = lax.dot_general(
            y * w, y, (((1,), (1,)), ((), ())), precision=lax.Precision.HIGHEST, preferred_element_type=F32
        )
        system = eye + gram * scale
        norm = jnp.sqrt(jnp.sum(system * system, keepdims=True))
        roots.append(system / norm)
        norms.append(norm)
        drive = jnp.sum(y * (w * (value_ref[p] - mean)), axis=1, keepdims=True) * scale
        drives.append(jnp.broadcast_to(drive, (members, members)))
    inverses = [None] * count
    for sweep in range(NS_ITERS):
        for p in range(count):
            s = halves(roots[p])
            if sweep == 0:
                newton = 1.5 * eye - 0.5 * roots[p]
                inverses[p] = newton
                n = halves(newton)
            else:
                z = halves(inverses[p])
                newton = 1.5 * eye - 0.5 * dot3(z, s)
                n = halves(newton)
                inverses[p] = dot3(n, z)
            if sweep < NS_ITERS - 1:
                roots[p] = dot3(s, n)
    for p in range(count):
        z = halves(inverses[p])
        mean_w = dot3(z, halves(dot3(z, halves(drives[p])))) / norms[p]
        out_ref[p] = inverses[p] / jnp.sqrt(norms[p]) + mean_w


def transforms(base, hx, chosen, weight, value):
    blocks, members, width = hx.shape
    count = chosen.shape[0]
    return pl.pallas_call(
        transform_kernel,
        in_specs=[pl.BlockSpec(memory_space=pltpu.SMEM)] + [pl.BlockSpec(memory_space=pltpu.VMEM)] * 4,
        out_specs=pl.BlockSpec(memory_space=pltpu.VMEM),
        out_shape=jax.ShapeDtypeStruct((count, members, members), F32),
        name="transforms",
    )(base, hx, chosen, weight, value)


def mix(transform, x):
    mean = jnp.mean(x, axis=0, keepdims=True)
    gh, gl = halves(transform.T)
    return mean + dot3((gh, gl), halves(x - mean))


def first_analysis_kernel(count, q_ref, g_ref, *refs):
    parts, out_ref = refs[:-1], refs[-1]
    tile = pl.program_id(0)
    for p in range(SUB // PR):
        patch = tile * (SUB // PR) + p
        g = g_ref[lax.bitwise_xor(patch // count, q_ref[0]), lax.rem(patch, count)]
        x = jnp.concatenate(
            [jnp.concatenate([part[:, PR * p + i, :] for part in parts], axis=0) for i in range(PR)], axis=1
        )
        y = mix(g, x)
        ny = parts[0].shape[2]
        for i in range(PR):
            out_ref[PR * p + i] = y[:, i * ny : (i + 1) * ny]


def first_analysis(q, g, parts):
    n, height, ny = parts[0].shape
    members = n * len(parts)
    return pl.pallas_call(
        functools.partial(first_analysis_kernel, g.shape[1]),
        grid=(height // SUB,),
        in_specs=[
            pl.BlockSpec(memory_space=pltpu.SMEM),
            pl.BlockSpec(g.shape, lambda i: (0, 0, 0, 0)),
        ]
        + [pl.BlockSpec((n, SUB, ny), lambda i: (0, i, 0))] * len(parts),
        out_specs=pl.BlockSpec((SUB, members, ny), lambda i: (i, 0, 0)),
        out_shape=jax.ShapeDtypeStruct((height, members, ny), F32),
        name="first_analysis",
    )(q, g, *parts)


def last_analysis_kernel(count, q_ref, g_ref, x_ref, *outs):
    tile = pl.program_id(0)
    n = outs[0].shape[0]
    ny = x_ref.shape[2]
    for p in range(SUB // PR):
        patch = tile * (SUB // PR) + p
        g = g_ref[lax.bitwise_xor(patch // count, q_ref[0]), lax.rem(patch, count)]
        x = jnp.concatenate([x_ref[PR * p + i] for i in range(PR)], axis=1)
        y = mix(g, x)
        for i in range(PR):
            for j, out in enumerate(outs):
                out[:, PR * p + i, :] = y[j * n : (j + 1) * n, i * ny : (i + 1) * ny]


def last_analysis(q, g, x, pieces):
    height, members, ny = x.shape
    n = members // pieces
    return pl.pallas_call(
        functools.partial(last_analysis_kernel, g.shape[1]),
        grid=(height // SUB,),
        in_specs=[
            pl.BlockSpec(memory_space=pltpu.SMEM),
            pl.BlockSpec(g.shape, lambda i: (0, 0, 0, 0)),
            pl.BlockSpec((SUB, members, ny), lambda i: (i, 0, 0)),
        ],
        out_specs=[pl.BlockSpec((n, SUB, ny), lambda i: (0, i, 0))] * pieces,
        out_shape=[jax.ShapeDtypeStruct((n, height, ny), F32)] * pieces,
        name="last_analysis",
    )(q, g, x)


def group_forecast_kernel(x_ref, lo_ref, hi_ref, coef_ref, pick_ref, out_ref, hx_ref, buf_q, buf_a, buf_b):
    height, mt, ny = x_ref.shape
    halo = lo_ref.shape[0]
    total = height + 2 * halo
    buf_q[:halo] = lo_ref[...]
    buf_q[halo : halo + height] = x_ref[...]
    buf_q[halo + height :] = hi_ref[...]

    def stage(src, lo, hi, write):
        def body(i, carry):
            prev, cur = carry
            nxt = src[i + 1]
            left = pltpu.roll(cur, ny - 1, 1)
            right = pltpu.roll(cur, 1, 1)
            k = [jnp.concatenate([coef_ref[c, i]] * (mt // SUB), axis=0) for c in range(5)]
            t = k[0] * cur + (k[1] * nxt + k[2] * prev) + (k[3] * left + k[4] * right)
            write(i, t)
            return cur, nxt

        lax.fori_loop(lo, hi, body, (src[lo - 1], src[lo]), unroll=2)

    def write_a(i, t):
        buf_a[i] = t

    def write_b(i, t):
        buf_b[i] = 0.75 * buf_q[i] + 0.25 * t

    def write_q(i, t):
        buf_q[i] = buf_q[i] * (1.0 / 3.0) + (2.0 / 3.0) * t

    for step in range(STEPS):
        e = 3 * step
        stage(buf_q, e + 1, total - e - 1, write_a)
        stage(buf_a, e + 2, total - e - 2, write_b)
        stage(buf_b, e + 3, total - e - 3, write_q)

    out_ref[...] = buf_q[halo : halo + height]
    block_rows = height // BLOCK
    per = pick_ref.shape[2]
    for b in range(block_rows):
        at = halo + BLOCK * b
        total_rows = (buf_q[at] + buf_q[at + 1]) + (buf_q[at + 2] + buf_q[at + 3])
        hi, mid, lo = thirds(total_rows)
        pick = pick_ref[b]
        hx_ref[:, b * per : (b + 1) * per] = bdot(hi, pick) + (bdot(mid, pick) + bdot(lo, pick))


def group_forecast(x, lo, hi, coef, pick):
    height, members, ny = x.shape
    halo = lo.shape[0]
    total = height + 2 * halo
    width = pick.shape[0] * pick.shape[2]
    return pl.pallas_call(
        group_forecast_kernel,
        grid=(members // MT,),
        in_specs=[
            pl.BlockSpec((height, MT, ny), lambda i: (0, i, 0)),
            pl.BlockSpec((halo, MT, ny), lambda i: (0, i, 0)),
            pl.BlockSpec((halo, MT, ny), lambda i: (0, i, 0)),
            pl.BlockSpec(coef.shape, lambda i: (0, 0, 0, 0)),
            pl.BlockSpec(pick.shape, lambda i: (0, 0, 0)),
        ],
        out_specs=[
            pl.BlockSpec((height, MT, ny), lambda i: (0, i, 0)),
            pl.BlockSpec((MT, width), lambda i: (i, 0)),
        ],
        out_shape=[
            jax.ShapeDtypeStruct((height, members, ny), F32),
            jax.ShapeDtypeStruct((members, width), F32),
        ],
        scratch_shapes=[pltpu.VMEM((total, MT, ny), F32)] * 3,
        name="group_forecast",
    )(x, lo, hi, coef, pick)


def local(n, ensemble, flow_speed, spreading, obs_values, obs_var, obs_block, readers, counts):
    mine, nv, nx, ny = ensemble.shape
    members = mine * n
    nobs = obs_var.shape[0]
    patches, slots = readers.shape
    groups = n // nv
    height = nx // groups
    count = patches // n
    width = nobs // n
    nbr, nbc = nx // BLOCK, ny // BLOCK
    per_row = nobs // nbr

    place = [2 * r if 2 * r < groups else 2 * (groups - 1 - r) + 1 for r in range(groups)]
    owner_rows = [place.index(g) for g in range(groups)]

    def device(r, q):
        return nv * place[r % groups] + q

    me = lax.axis_index("dev")
    q = lax.rem(me, nv)
    g = me // nv
    r = jnp.where(g % 2 == 0, g // 2, groups - 1 - g // 2) if groups > 1 else g * 0
    spot = r * nv + q
    q_ref = q.reshape(1).astype(jnp.int32)

    obs_col = obs_block % nbc
    obs_v = obs_block // (nbr * nbc)
    lanes = max(128, nbc)
    col_table = jnp.pad(obs_col.reshape(nbr, per_row), ((0, 0), (0, lanes - per_row)))
    var_table = jnp.pad(obs_v.reshape(nbr, per_row), ((0, 0), (0, lanes - per_row)))

    first = spot * count
    chosen = lax.dynamic_slice_in_dim(readers, first, count, 0)
    my_counts = lax.dynamic_slice_in_dim(counts, first, count, 0)
    patch_index = first + jnp.arange(count, dtype=jnp.int32)
    obs_row = (chosen * nbr // nobs).astype(F32) * BLOCK + 0.5 * (BLOCK - 1)
    patch_row = patch_index.astype(F32) * PR + 0.5 * (PR - 1)
    gap = jnp.abs(obs_row - patch_row[:, None])
    distance = jnp.minimum(gap, nx - gap)
    taper = jnp.exp(-0.5 * (distance / TAPER_ROWS) ** 2)
    listed = jnp.arange(slots, dtype=jnp.int32) < my_counts[:, None]
    weight = jnp.where(listed, taper / obs_var[chosen], 0.0)[:, None, :]
    chosen_rows = chosen[:, None, :]

    rows = lax.rem(r * height - HALO + jnp.arange(height + 2 * HALO, dtype=jnp.int32) + nx, nx)
    doubled = lambda a: jnp.concatenate([a, a, a], axis=-2)
    start = r * height - HALO + nx
    take = lambda a: lax.dynamic_slice_in_dim(doubled(a), start, height + 2 * HALO, a.ndim - 2)
    my_flow = 0.5 * take(flow_speed)
    my_spread = take(lax.dynamic_index_in_dim(spreading, q, 0, keepdims=False))
    coef = jnp.stack(
        [
            1.0 - 4.0 * my_spread,
            my_spread - my_flow[0],
            my_spread + my_flow[0],
            my_spread - my_flow[1],
            my_spread + my_flow[1],
        ]
    )
    coef = jnp.broadcast_to(coef[:, :, None, :], coef.shape[:2] + (SUB, ny))
    block_rows = height // BLOCK
    group_col = lax.dynamic_slice_in_dim(obs_col.reshape(nbr, per_row), r * block_rows, block_rows, 0)
    group_var = lax.dynamic_slice_in_dim(obs_v.reshape(nbr, per_row), r * block_rows, block_rows, 0)
    column = jnp.arange(ny, dtype=jnp.int32) // BLOCK
    pick = jnp.where(
        (column[None, :, None] == group_col[:, None, :]) & (group_var[:, None, :] == q),
        1.0 / (BLOCK * BLOCK),
        0.0,
    ).astype(BF16)

    def solve(cycle, hx):
        every = lax.all_to_all(jnp.broadcast_to(hx[None], (n,) + hx.shape), "dev", 0, 0, tiled=True)
        base = jnp.array([(owner_rows[d // nv] * nv + d % nv) * width for d in range(n)], jnp.int32)
        value = obs_values[cycle][chosen][:, None, :]
        own = transforms(base, every, chosen_rows, weight, value)
        stacked = [own]
        for c in range(1, nv):
            pairs = [(nv * b + i, nv * b + (i ^ c)) for b in range(groups) for i in range(nv)]
            stacked.append(lax.ppermute(own, "dev", pairs))
        return jnp.stack(stacked)

    arrived, observed = [], []
    for j in range(mine):
        fields, hx = member_forecast(j, ensemble, flow_speed, spreading, col_table, var_table, owner_rows)
        arrived.append(lax.all_to_all(fields.reshape(n, height, ny), "dev", 0, 0, tiled=True))
        observed.append(hx[:, :per_row].reshape(groups, nv, width))
    observed = jnp.stack(observed, 2)
    observed = jnp.concatenate([observed[r0 : r0 + 1] for r0 in owner_rows], 0).reshape(n, mine, width)
    observed = lax.all_to_all(observed, "dev", 0, 0, tiled=True)
    hx = observed.transpose(1, 0, 2).reshape(members, width)
    state = first_analysis(q_ref, solve(0, hx), arrived)

    lo, hi = [], []
    left = HALO
    hop = 1
    while left > 0:
        rows_k = min(left, height)
        up = [(device(r0, i), device(r0 + hop, i)) for r0 in range(groups) for i in range(nv)]
        down = [(b, a) for a, b in up]
        lo.insert(0, lax.ppermute(state[height - rows_k :], "dev", up))
        hi.append(lax.ppermute(state[:rows_k], "dev", down))
        left -= rows_k
        hop += 1
    lo = lo[0] if len(lo) == 1 else jnp.concatenate(lo, 0)
    hi = hi[0] if len(hi) == 1 else jnp.concatenate(hi, 0)
    state, partial = group_forecast(state, lo, hi, coef, pick)
    partial = partial.reshape(members, nv, width)
    pieces = [lax.dynamic_index_in_dim(partial, q, 1, keepdims=False)]
    for c in range(1, nv):
        pairs = [(nv * b + i, nv * b + (i ^ c)) for b in range(groups) for i in range(nv)]
        other = lax.dynamic_index_in_dim(partial, lax.bitwise_xor(q, c), 1, keepdims=False)
        pieces.append(lax.ppermute(other, "dev", pairs))
    hx = functools.reduce(lambda a, b: a + b, pieces)
    outs = last_analysis(q_ref, solve(1, hx), state, mine)
    final = []
    for out in outs:
        back = lax.all_to_all(out, "dev", 0, 0, tiled=True).reshape(groups, nv, height, ny)
        back = jnp.concatenate([back[place[r0]][:, None] for r0 in range(groups)], 1)
        final.append(back.reshape(nv, nx, ny))
    return jnp.stack(final)


def solution(mesh):
    n = mesh.shape["dev"]
    return jax.shard_map(
        functools.partial(local, n),
        mesh=mesh,
        in_specs=(P("dev", None, None, None), P(), P(), P(), P(), P(), P(), P()),
        out_specs=P("dev", None, None, None),
        check_vma=False,
    )
```

time: 1150 us -> 746 us (0.65); the launches traced: 1130 us -> 744 us
  local copies, waits for them, and re-layouts: 539 us -> 41.1 us
  Pallas kernels: 0 us -> 316 us
  other arithmetic: 244 us -> 10.5 us
  waiting for transfers between devices: 43.3 us -> 238 us
  blocking collectives: 194 us -> 103 us
  matrix products: 51.8 us -> 0 us
  between operations: 17.5 us -> 0.59 us
    concatenate x280 -> x10, local copies, waits for them, and re-layouts: 360 us -> 7.23 us  [the longest x8 7.17 us: local(): jnp.concatenate([back[place[r0]][:, None] for r0 in range(groups)], 1)]
    pallas_call x0 -> x9, Pallas kernels: none -> 316 us  [the longest x1 135 us: group_forecast(): pl.pallas_call(group_forecast_kernel, grid=(members // MT,), in_specs=[pl...]
    add x81 -> x2, other arithmetic: 223 us -> 0.02 us  [the longest x1 0.02 us: local(): hx = functools.reduce(lambda a, b: a + b, pieces)]
    all_to_all x8 -> x7, waiting for transfers between devices: 43.2 us -> 184 us  [the longest x2 92.3 us: solve(): lax.all_to_all(jnp.broadcast_to(hx[None], (n,) + hx.shape), 'dev', 0, 0,...]
    all_to_all x2 -> x4, blocking collectives: 194 us -> 103 us  [the longest x2 58.2 us: local(): lax.all_to_all(fields.reshape(n, height, ny), 'dev', 0, 0, tiled=True)]
    ppermute x0 -> x11, waiting for transfers between devices: none -> 54 us  [the longest x1 24.8 us: local(): hi.append(lax.ppermute(state[:rows_k], 'dev', down))]
    dot_general x72 -> x0, matrix products: 51.8 us -> none  [the longest x20 13.3 us: sweep_once(): jnp.einsum('pij,pjk->pik', inv_root, root_up, precision=EXACT_DOT)]
    gather x10 -> x3, local copies, waits for them, and re-layouts: 51.6 us -> 11.7 us  [the longest x2 8.6 us: solve(): value = obs_values[cycle][chosen][:, None, :]]
  transfers between devices with their start and end apart: 10 -> 18, of which waited for: 4 -> 14; matrix products, arithmetic and copies ran while one was open for 41% -> 4% of each run, Pallas kernels for 0% -> 3%
where the time goes in v1:
time: 746 us; the launch traced here: 744 us
  Pallas kernels  316 us (42%)
  waiting for transfers between devices  238 us (32%)
  blocking collectives  103 us (14%)
  local copies, waits for them, and re-layouts  41.1 us (6%)
  starting transfers between devices  34.5 us (5%)
  other arithmetic  10.5 us (1%)
    pallas_call x1, Pallas kernels, group_forecast(): pl.pallas_call(group_forecast_kernel, grid=(members // MT,), in_specs=[pl...  135 us
    pallas_call x4, Pallas kernels, member_forecast(): pl.pallas_call(functools.partial(member_forecast_kernel, owner_rows), gri...  127 us
    all_to_all x2, waiting for transfers between devices, solve(): lax.all_to_all(jnp.broadcast_to(hx[None], (n,) + hx.shape), 'dev', 0, 0,...  92.3 us
    all_to_all x3, waiting for transfers between devices, local(): lax.all_to_all(out, 'dev', 0, 0, tiled=True).reshape(groups, nv, height, ny)  65.9 us
    all_to_all x2, blocking collectives, local(): lax.all_to_all(fields.reshape(n, height, ny), 'dev', 0, 0, tiled=True)  58.2 us
    pallas_call x2, Pallas kernels, transforms(): pl.pallas_call(transform_kernel, in_specs=[pl.BlockSpec(memory_space=pltp...  40 us
    all_to_all x1, blocking collectives, local(): lax.all_to_all(out, 'dev', 0, 0, tiled=True).reshape(groups, nv, height, ny)  30.3 us
    all_to_all x2, waiting for transfers between devices, local(): lax.all_to_all(fields.reshape(n, height, ny), 'dev', 0, 0, tiled=True)  26.2 us
  transfers between devices with their start and end apart: 18, of which 14 were waited for; matrix products, arithmetic and copies ran while one was open for 4% of the time, Pallas kernels for 3%

profile of v1, /device:TPU:0, one launch (start us, length us, event | category | flops | bytes accessed | tf_op | source)
XLA Modules:
  0.0 744.5 jit_solution(18392187411097053804)
XLA Ops:
  2.1 31.7 %member_forecast.7 = (f32[8,4,32,256]{3,2,1,0:T(8,128)}, f32[64,128]{1,0:T(8,128)}) custom-call(f32[4,4,256,256]{3,2,1,0:T(8,128)} %q_ref.7, f32[2,256,256]{2,1,0:T(8,128)} %flow_ref.7, f32[4,256,256]{2,1,0:T(8,128)} %spread_ref.7, s32[64,128]{1,0:T(8,128)} %pad.7.col_ref, s32[64,128]{1,0:T(8,128)} %pad.8.var_ref), custom_call_target="tpu_custom_call" | custom-call | tf_op jit(solution)/shard_map/member_forecast/pallas_call | solution.py:151
  33.8 31.7 %member_forecast.6 = (f32[8,4,32,256]{3,2,1,0:T(8,128)}, f32[64,128]{1,0:T(8,128)}) custom-call(f32[4,4,256,256]{3,2,1,0:T(8,128)} %q_ref.7, f32[2,256,256]{2,1,0:T(8,128)} %flow_ref.7, f32[4,256,256]{2,1,0:T(8,128)} %spread_ref.7, s32[64,128]{1,0:T(8,128)} %pad.7.col_ref, s32[64,128]{1,0:T(8,128)} %pad.8.var_ref), custom_call_target="tpu_custom_call" | custom-call | tf_op jit(solution)/shard_map/member_forecast/pallas_call | solution.py:151
  65.5 31.7 %member_forecast.5 = (f32[8,4,32,256]{3,2,1,0:T(8,128)}, f32[64,128]{1,0:T(8,128)}) custom-call(f32[4,4,256,256]{3,2,1,0:T(8,128)} %q_ref.7, f32[2,256,256]{2,1,0:T(8,128)} %flow_ref.7, f32[4,256,256]{2,1,0:T(8,128)} %spread_ref.7, s32[64,128]{1,0:T(8,128)} %pad.7.col_ref, s32[64,128]{1,0:T(8,128)} %pad.8.var_ref), custom_call_target="tpu_custom_call" | custom-call | tf_op jit(solution)/shard_map/member_forecast/pallas_call | solution.py:151
  97.3 31.8 %member_forecast.4 = (f32[8,4,32,256]{3,2,1,0:T(8,128)}, f32[64,128]{1,0:T(8,128)}) custom-call(f32[4,4,256,256]{3,2,1,0:T(8,128)} %q_ref.7, f32[2,256,256]{2,1,0:T(8,128)} %flow_ref.7, f32[4,256,256]{2,1,0:T(8,128)} %spread_ref.7, s32[64,128]{1,0:T(8,128)} %pad.7.col_ref, s32[64,128]{1,0:T(8,128)} %pad.8.var_ref), custom_call_target="tpu_custom_call" | custom-call | tf_op jit(solution)/shard_map/member_forecast/pallas_call | solution.py:151
  130.5 14.5 %all_to_all.55 = f32[32,4,128]{2,1,0:T(4,128)S(1)} all-to-all(f32[32,4,128]{2,1,0:T(4,128)S(1)} %bitcast.205), channel_id=1, replica_groups=mesh['dev'=32] {'dev'}, dimensions={0} | all-to-all | bytes 131072 | tf_op jit(solution)/shard_map/all_to_all | solution.py:471
  145.0 28.6 %all_to_all.56.refs_3_ = f32[32,32,256]{2,1,0:T(8,128)} all-to-all(f32[32,32,256]{2,1,0:T(8,128)S(1)} %bitcast.200), channel_id=1, replica_groups=mesh['dev'=32] {'dev'}, dimensions={0} | all-to-all | bytes 2097152 | tf_op jit(solution)/shard_map/all_to_all | solution.py:467
  173.6 29.6 %all_to_all.57.refs_2_ = f32[32,32,256]{2,1,0:T(8,128)} all-to-all(f32[32,32,256]{2,1,0:T(8,128)S(1)} %bitcast.201), channel_id=1, replica_groups=mesh['dev'=32] {'dev'}, dimensions={0} | all-to-all | bytes 2097152 | tf_op jit(solution)/shard_map/all_to_all | solution.py:467
  203.2 3.6 all-to-all-start.3
  206.9 26.2 %all-to-all-done.3.refs_1_ = f32[32,32,256]{2,1,0:T(8,128)S(1)} async-done(((f32[32,32,256]{2,1,0:T(8,128)}), f32[32,32,256]{2,1,0:T(8,128)S(1)}, u32[]{:S(2)}, u32[]{:S(2)}) %all-to-all-start.3) | async-done | bytes 1048608 | tf_op jit(solution)/shard_map/all_to_all | solution.py:467
  233.1 1.7 broadcast_in_dim.55
  234.7 3.6 all-to-all-start.1
  239.2 47.9 %all-to-all-done.1.hx_ref = f32[32,128,128]{2,1,0:T(8,128)S(1)} async-done(((f32[32,128,128]{2,1,0:T(8,128)}), f32[32,128,128]{2,1,0:T(8,128)S(1)}, u32[]{:S(2)}, u32[]{:S(2)}) %all-to-all-start.1) | async-done | bytes 2097184 | tf_op jit(solution)/shard_map/all_to_all | solution.py:454
  287.1 4.3 all-to-all-start.2
  291.4 3.1 gather_fusion
  294.6 4.3 gather_fusion.1
  300.6 20.0 %transforms.2 = f32[4,128,128]{2,1,0:T(8,128)} custom-call(s32[32]{0:T(128)} %constant.151.clone.base_ref, f32[32,128,128]{2,1,0:T(8,128)} %copy-done.2, s32[4,1,128]{2,1,0:T(1,128)} %bitcast.216, f32[4,1,128]{2,1,0:T(1,128)} %bitcast.222, f32[4,1,128]{2,1,0:T(1,128)} %bitcast.224), custom_call_target="tpu_custom_call" | custom-call | tf_op jit(solution)/shard_map/transforms/pallas_call | solution.py:230
  320.7 1.3 collective-permute-start.2
  323.3 6.0 collective-permute-done.2
  329.2 5.9 collective-permute-done.1
  335.1 2.0 pad_maximum_fusion.1.g_ref
  338.1 7.1 first_analysis.1.x_ref
  345.2 3.3 fusion.49
  348.5 1.6 collective-permute-start.4
  351.7 24.8 %collective-permute-done.4.hi_ref = f32[9,128,256]{2,1,0:T(8,128)S(1)} collective-permute-done((f32[9,128,256]{2,1,0:T(8,128)}, f32[9,128,256]{2,1,0:T(8,128)S(1)}, u32[]{:S(2)}, u32[]{:S(2)}) %collective-permute-start.4) | collective-permute-done | bytes 1179680 | tf_op jit(solution)/shard_map/ppermute | solution.py:483
  377.7 1.7 broadcast_in_dim.61.coef_ref
  379.5 135.5 %group_forecast.1 = (f32[32,128,256]{2,1,0:T(8,128)}, f32[128,512]{1,0:T(8,128)}) custom-call(f32[32,128,256]{2,1,0:T(8,128)} %first_analysis.1.x_ref, f32[9,128,256]{2,1,0:T(8,128)} %copy-done.11, f32[9,128,256]{2,1,0:T(8,128)} %copy-done.10, f32[5,50,8,256]{3,2,1,0:T(8,128)} %broadcast_in_dim.61.coef_ref, bf16[8,256,64]{2,1,0:T(8,128)(2,1)} %select_convert_fusion.pick_ref), custom_call_target="tpu_custom_call" | custom-call | tf_op jit(solution)/shard_map/group_forecast/pallas_call | solution.py:360
  516.3 1.6 collective-permute-start.5
  518.4 2.2 collective-permute-done.7
  520.6 1.5 collective-permute-done.6
  522.1 1.6 broadcast_in_dim.64
  523.7 4.2 all-to-all-start.6
  527.8 4.3 gather_fusion.2
  532.2 44.4 %all-to-all-done.6.hx_ref = f32[32,128,128]{2,1,0:T(8,128)S(1)} async-done(((f32[32,128,128]{2,1,0:T(8,128)}), f32[32,128,128]{2,1,0:T(8,128)S(1)}, u32[]{:S(2)}, u32[]{:S(2)}) %all-to-all-start.6) | async-done | bytes 2097184 | tf_op jit(solution)/shard_map/all_to_all | solution.py:454
  577.8 20.0 %transforms.3 = f32[4,128,128]{2,1,0:T(8,128)} custom-call(s32[32]{0:T(128)} %constant.151.clone.base_ref, f32[32,128,128]{2,1,0:T(8,128)} %copy-done.3, s32[4,1,128]{2,1,0:T(1,128)} %bitcast.217, f32[4,1,128]{2,1,0:T(1,128)} %bitcast.223, f32[4,1,128]{2,1,0:T(1,128)} %bitcast.225), custom_call_target="tpu_custom_call" | custom-call | tf_op jit(solution)/shard_map/transforms/pallas_call | solution.py:230
  599.7 7.0 collective-permute-done.10
  606.7 5.4 collective-permute-done.9
  612.1 2.0 pad_maximum_fusion.2.g_ref
  614.1 6.8 last_analysis.1
  621.0 30.3 %all_to_all.58 = f32[32,32,256]{2,1,0:T(8,128)S(1)} all-to-all(f32[32,32,256]{2,1,0:T(8,128)} %get-tuple-element.32), channel_id=1, replica_groups=mesh['dev'=32] {'dev'}, dimensions={0} | all-to-all | bytes 2097152 | tf_op jit(solution)/shard_map/all_to_all | solution.py:499
  651.3 3.6 all-to-all-start.9
  655.1 26.1 %all-to-all-done.9 = f32[32,32,256]{2,1,0:T(8,128)S(1)} async-done(((f32[32,32,256]{2,1,0:T(8,128)}), f32[32,32,256]{2,1,0:T(8,128)S(1)}, u32[]{:S(2)}, u32[]{:S(2)}) %all-to-all-start.9) | async-done | bytes 1048608 | tf_op jit(solution)/shard_map/all_to_all | solution.py:499
  681.1 3.6 all-to-all-start.8
  686.1 2.3 copy.25
  693.1 17.9 %all-to-all-done.8 = f32[32,32,256]{2,1,0:T(8,128)S(1)} async-done(((f32[32,32,256]{2,1,0:T(8,128)}), f32[32,32,256]{2,1,0:T(8,128)S(1)}, u32[]{:S(2)}, u32[]{:S(2)}) %all-to-all-start.8) | async-done | bytes 1048608 | tf_op jit(solution)/shard_map/all_to_all | solution.py:499
  711.0 3.6 all-to-all-start.7
  715.3 2.3 copy.24
  718.8 22.0 %all-to-all-done.7 = f32[32,32,256]{2,1,0:T(8,128)S(1)} async-done(((f32[32,32,256]{2,1,0:T(8,128)}), f32[32,32,256]{2,1,0:T(8,128)S(1)}, u32[]{:S(2)}, u32[]{:S(2)}) %all-to-all-start.7) | async-done | bytes 1048608 | tf_op jit(solution)/shard_map/all_to_all | solution.py:499
  742.0 2.4 pad_maximum_fusion
  (131 shorter events, 25.3 us)
Async XLA Ops:
  0.0 291.4 %copy-start = (f32[4096]{0:T(1024)S(1)}, f32[4096]{0:T(1024)}, u32[]{:S(2)}) copy-start(f32[4096]{0:T(1024)} %param.14) | copy-start | bytes 49156
  97.3 31.9 %copy-start.16 = (f32[64,128]{1,0:T(8,128)S(1)}, f32[64,128]{1,0:T(8,128)}, u32[]{:S(2)}) copy-start(f32[64,128]{1,0:T(8,128)} %get-tuple-element.22) | copy-start | bytes 98308
  97.3 31.9 %copy-start.17 = (f32[64,128]{1,0:T(8,128)S(1)}, f32[64,128]{1,0:T(8,128)}, u32[]{:S(2)}) copy-start(f32[64,128]{1,0:T(8,128)} %get-tuple-element.21) | copy-start | bytes 98308
  97.3 32.0 %copy-start.18 = (f32[64,128]{1,0:T(8,128)S(1)}, f32[64,128]{1,0:T(8,128)}, u32[]{:S(2)}) copy-start(f32[64,128]{1,0:T(8,128)} %get-tuple-element.20) | copy-start | bytes 98308
  97.3 47.7 %copy-start.12 = (f32[8,4,32,256]{3,2,1,0:T(8,128)S(1)}, f32[8,4,32,256]{3,2,1,0:T(8,128)}, u32[]{:S(2)}) copy-start(f32[8,4,32,256]{3,2,1,0:T(8,128)} %get-tuple-element.26) | copy-start | bytes 3145732
  129.1 44.5 %copy-start.13 = (f32[8,4,32,256]{3,2,1,0:T(8,128)S(1)}, f32[8,4,32,256]{3,2,1,0:T(8,128)}, u32[]{:S(2)}) copy-start(f32[8,4,32,256]{3,2,1,0:T(8,128)} %get-tuple-element.25) | copy-start | bytes 3145732
  203.2 29.8 %all-to-all-start.3 = ((f32[32,32,256]{2,1,0:T(8,128)}), f32[32,32,256]{2,1,0:T(8,128)S(1)}, u32[]{:S(2)}, u32[]{:S(2)}) async-start(f32[32,32,256]{2,1,0:T(8,128)} %bitcast.15), calls=%async_computation.3 | async-start | bytes 2097152 | tf_op jit(solution)/shard_map/all_to_all | solution.py:467
  233.1 1.7 copy-start.4
  234.7 3.7 copy-start.20
  234.7 52.4 %all-to-all-start.1 = ((f32[32,128,128]{2,1,0:T(8,128)}), f32[32,128,128]{2,1,0:T(8,128)S(1)}, u32[]{:S(2)}, u32[]{:S(2)}) async-start(f32[32,128,128]{2,1,0:T(8,128)} %broadcast_in_dim.55), calls=%async_computation.1 | async-start | bytes 4194304 | tf_op jit(solution)/shard_map/all_to_all | solution.py:454
  239.2 60.8 %copy-start.15 = (s32[4,128]{1,0:T(4,128)}, s32[4,128]{1,0:T(4,128)S(1)}, u32[]{:S(2)}) copy-start(s32[4,128]{1,0:T(4,128)S(1)} %get-tuple-element.36) | copy-start | bytes 6148
  287.1 7.5 %copy-start.2 = (f32[32,128,128]{2,1,0:T(8,128)}, f32[32,128,128]{2,1,0:T(8,128)S(1)}, u32[]{:S(2)}) copy-start(f32[32,128,128]{2,1,0:T(8,128)S(1)} %all-to-all-done.1.hx_ref) | copy-start | bytes 6291460
  287.1 7.5 %copy-start.19 = (f32[2,4096]{1,0:T(2,128)S(1)}, f32[2,4096]{1,0:T(2,128)}, u32[]{:S(2)}) copy-start(f32[2,4096]{1,0:T(2,128)} %param.13) | copy-start | bytes 98308
  287.1 50.0 %all-to-all-start.2 = ((f32[32,32,256]{2,1,0:T(8,128)}), f32[32,32,256]{2,1,0:T(8,128)S(1)}, u32[]{:S(2)}, u32[]{:S(2)}) async-start(f32[32,32,256]{2,1,0:T(8,128)} %bitcast.199), calls=%async_computation.2 | async-start | bytes 2097152 | tf_op jit(solution)/shard_map/all_to_all | solution.py:467
  298.9 24.3 %copy-start.1 = (f32[2,256,256]{2,1,0:T(8,128)S(1)}, f32[2,256,256]{2,1,0:T(8,128)}, u32[]{:S(2)}) copy-start(f32[2,256,256]{2,1,0:T(8,128)} %flow_ref.7) | copy-start | bytes 1572868
  320.7 8.6 %collective-permute-start.2 = (f32[4,128,128]{2,1,0:T(8,128)}, f32[4,128,128]{2,1,0:T(8,128)S(1)}, u32[]{:S(2)}, u32[]{:S(2)}) collective-permute-start(f32[4,128,128]{2,1,0:T(8,128)} %transforms.2), channel_id=1, source_target_pairs={{0,3},{1,2},{2,1},{3,0},{4,7},{5,6},{6,5},{7,4},{8,11},{9,10},{10,... | collective-permute-start | bytes 786440 | tf_op jit(solution)/shard_map/ppermute | solution.py:461
  322.0 13.1 %collective-permute-start.1 = (f32[4,128,128]{2,1,0:T(8,128)}, f32[4,128,128]{2,1,0:T(8,128)S(1)}, u32[]{:S(2)}, u32[]{:S(2)}) collective-permute-start(f32[4,128,128]{2,1,0:T(8,128)} %transforms.2), channel_id=1, source_target_pairs={{0,2},{1,3},{2,0},{3,1},{4,6},{5,7},{6,4},{7,5},{8,10},{9,11},{10,... | collective-permute-start | bytes 786440 | tf_op jit(solution)/shard_map/ppermute | solution.py:461
  322.4 12.7 %collective-permute-start = (f32[4,128,128]{2,1,0:T(8,128)}, f32[4,128,128]{2,1,0:T(8,128)S(1)}, u32[]{:S(2)}, u32[]{:S(2)}) collective-permute-start(f32[4,128,128]{2,1,0:T(8,128)} %transforms.2), channel_id=1, source_target_pairs={{0,1},{1,0},{2,3},{3,2},{4,5},{5,4},{6,7},{7,6},{8,9},{9,8},{10,11... | collective-permute-start | bytes 786440 | tf_op jit(solution)/shard_map/ppermute | solution.py:461
  337.1 1.0 copy-start.5
  345.2 5.3 copy-start.14
  348.5 27.9 %collective-permute-start.4 = (f32[9,128,256]{2,1,0:T(8,128)}, f32[9,128,256]{2,1,0:T(8,128)S(1)}, u32[]{:S(2)}, u32[]{:S(2)}) collective-permute-start(f32[9,128,256]{2,1,0:T(8,128)} %get-tuple-element.37), channel_id=1, source_target_pairs={{8,0},{9,1},{10,2},{11,3},{16,8},{17,9},{18,10},{19,11},{24,16},{2... | collective-permute-start | bytes 3538952 | tf_op jit(solution)/shard_map/ppermute | solution.py:483
  350.1 27.6 %collective-permute-start.3 = (f32[9,128,256]{2,1,0:T(8,128)}, f32[9,128,256]{2,1,0:T(8,128)S(1)}, u32[]{:S(2)}, u32[]{:S(2)}) collective-permute-start(f32[9,128,256]{2,1,0:T(8,128)} %get-tuple-element.38), channel_id=1, source_target_pairs={{0,8},{1,9},{2,10},{3,11},{8,16},{9,17},{10,18},{11,19},{16,24},{1... | collective-permute-start | bytes 3538952 | tf_op jit(solution)/shard_map/ppermute | solution.py:482
  376.5 3.0 copy-start.10
  377.7 1.7 copy-start.11
  516.2 4.4 collective-permute-start.7
  516.3 4.4 collective-permute-start.5
  517.8 4.3 collective-permute-start.6
  523.7 52.8 %all-to-all-start.6 = ((f32[32,128,128]{2,1,0:T(8,128)}), f32[32,128,128]{2,1,0:T(8,128)S(1)}, u32[]{:S(2)}, u32[]{:S(2)}) async-start(f32[32,128,128]{2,1,0:T(8,128)} %broadcast_in_dim.64), calls=%async_computation.6 | async-start | bytes 4194304 | tf_op jit(solution)/shard_map/all_to_all | solution.py:454
  576.5 1.3 copy-start.3
  597.9 8.8 %collective-permute-start.10 = (f32[4,128,128]{2,1,0:T(8,128)}, f32[4,128,128]{2,1,0:T(8,128)S(1)}, u32[]{:S(2)}, u32[]{:S(2)}) collective-permute-start(f32[4,128,128]{2,1,0:T(8,128)} %transforms.3), channel_id=1, source_target_pairs={{0,3},{1,2},{2,1},{3,0},{4,7},{5,6},{6,5},{7,4},{8,11},{9,10},{10,... | collective-permute-start | bytes 786440 | tf_op jit(solution)/shard_map/ppermute | solution.py:461
  598.4 13.7 %collective-permute-start.9 = (f32[4,128,128]{2,1,0:T(8,128)}, f32[4,128,128]{2,1,0:T(8,128)S(1)}, u32[]{:S(2)}, u32[]{:S(2)}) collective-permute-start(f32[4,128,128]{2,1,0:T(8,128)} %transforms.3), channel_id=1, source_target_pairs={{0,2},{1,3},{2,0},{3,1},{4,6},{5,7},{6,4},{7,5},{8,10},{9,11},{10,... | collective-permute-start | bytes 786440 | tf_op jit(solution)/shard_map/ppermute | solution.py:461
  599.2 12.9 %collective-permute-start.8 = (f32[4,128,128]{2,1,0:T(8,128)}, f32[4,128,128]{2,1,0:T(8,128)S(1)}, u32[]{:S(2)}, u32[]{:S(2)}) collective-permute-start(f32[4,128,128]{2,1,0:T(8,128)} %transforms.3), channel_id=1, source_target_pairs={{0,1},{1,0},{2,3},{3,2},{4,5},{5,4},{6,7},{7,6},{8,9},{9,8},{10,11... | collective-permute-start | bytes 786440 | tf_op jit(solution)/shard_map/ppermute | solution.py:461
  651.3 29.8 %all-to-all-start.9 = ((f32[32,32,256]{2,1,0:T(8,128)}), f32[32,32,256]{2,1,0:T(8,128)S(1)}, u32[]{:S(2)}, u32[]{:S(2)}) async-start(f32[32,32,256]{2,1,0:T(8,128)} %get-tuple-element.31), calls=%async_computation.9 | async-start | bytes 2097152 | tf_op jit(solution)/shard_map/all_to_all | solution.py:499
  655.0 26.1 %copy-start.9 = (f32[4,8,32,256]{3,2,0,1:T(8,128)}, f32[4,8,32,256]{3,2,0,1:T(8,128)S(1)}, u32[]{:S(2)}) copy-start(f32[4,8,32,256]{3,2,0,1:T(8,128)S(1)} %fusion.2) | copy-start | bytes 3145732
  681.1 29.8 %all-to-all-start.8 = ((f32[32,32,256]{2,1,0:T(8,128)}), f32[32,32,256]{2,1,0:T(8,128)S(1)}, u32[]{:S(2)}, u32[]{:S(2)}) async-start(f32[32,32,256]{2,1,0:T(8,128)} %get-tuple-element.30), calls=%async_computation.8 | async-start | bytes 2097152 | tf_op jit(solution)/shard_map/all_to_all | solution.py:499
  711.0 29.8 %all-to-all-start.7 = ((f32[32,32,256]{2,1,0:T(8,128)}), f32[32,32,256]{2,1,0:T(8,128)S(1)}, u32[]{:S(2)}, u32[]{:S(2)}) async-start(f32[32,32,256]{2,1,0:T(8,128)} %get-tuple-element.29), calls=%async_computation.7 | async-start | bytes 2097152 | tf_op jit(solution)/shard_map/all_to_all | solution.py:499
  718.8 22.2 %copy-start.6 = (f32[4,8,32,256]{3,2,1,0:T(8,128)S(1)}, f32[4,8,32,256]{3,2,1,0:T(8,128)}, u32[]{:S(2)}) copy-start(f32[4,8,32,256]{3,2,1,0:T(8,128)} %copy.25) | copy-start | bytes 3145732
  718.8 22.2 %copy-start.7 = (f32[4,8,32,256]{3,2,1,0:T(8,128)S(1)}, f32[4,8,32,256]{3,2,1,0:T(8,128)}, u32[]{:S(2)}) copy-start(f32[4,8,32,256]{3,2,1,0:T(8,128)} %copy.24) | copy-start | bytes 3145732
  740.8 1.2 copy-start.8

commit v2 on v1

v2 whole, which is shorter than its diff:
```python
import functools

import jax
import jax.numpy as jnp
from jax import lax
from jax.experimental import pallas as pl
from jax.experimental.pallas import tpu as pltpu
from jax.sharding import PartitionSpec as P

PR = 2
BLOCK = 4
STEPS = 3
CYCLES = 2
NS_ITERS = 10
TAPER_ROWS = 6.0
HALO = 3 * STEPS
SUB = 8
NEAR = 3
SCALES = (1.0 / 3.0, 0.5, 1.0)
F32 = jnp.float32
BF16 = jnp.bfloat16


def exact_dot(a, b):
    return jnp.dot(a, b, precision=lax.Precision.HIGHEST, preferred_element_type=F32)


def halves(x):
    hi = x.astype(BF16)
    return hi, (x - hi.astype(F32)).astype(BF16)


def thirds(x):
    hi = x.astype(BF16)
    rest = x - hi.astype(F32)
    mid = rest.astype(BF16)
    return hi, mid, (rest - mid.astype(F32)).astype(BF16)


def bdot(a, b):
    return jnp.dot(a, b, preferred_element_type=F32)


def dot3(a, b):
    (ah, al), (bh, bl) = a, b
    return bdot(ah, bh) + (bdot(ah, bl) + bdot(al, bh))


def stencil(src, base, coef, at, lo, hi, rb, unroll, write):
    copies = src.shape[1] // SUB
    half = src.shape[2] // 2

    def k(c, rows):
        v = coef[at + c, rows]
        return v if copies == 1 else jnp.concatenate([v] * copies, axis=1)

    def body(t, _):
        i = lo + t * rb
        rows = pl.ds(i, rb)
        x = src[pl.ds(i - 1, rb + 2)]
        cur, up, dn = x[1:-1], x[2:], x[:-2]
        even, odd = cur[..., :half], cur[..., half:]
        left = jnp.concatenate([odd, pltpu.roll(even, half - 1, 2)], axis=2)
        right = jnp.concatenate([pltpu.roll(odd, 1, 2), even], axis=2)
        total = (k(0, rows) * cur + (k(1, rows) * up + k(2, rows) * dn)) + (
            k(3, rows) * left + k(4, rows) * right
        )
        write[rows] = total if base is None else base[rows] + total
        return 0

    n = -(-(hi - lo) // rb)
    lax.fori_loop(0, n, body, 0, unroll=min(unroll, n))


def store_coefs(coef, rows, spread, fx, fy):
    parts = (-4.0 * spread, spread - fx, spread + fx, spread - fy, spread + fy)
    for s, scale in enumerate(SCALES):
        for c, part in enumerate(parts):
            v = part if scale == 1.0 else scale * part
            coef[5 * s + c, rows] = 1.0 + v if (s == 0 and c == 0) else v


def lane_gather(x, idx):
    return jnp.take_along_axis(x, idx, axis=1, mode="promise_in_bounds")


def strided(nat, t, t_rows):
    a, b = (nat[h, pl.ds(t, SUB, stride=t_rows), :] for h in range(2))
    half = a.shape[1]
    lane = lax.broadcasted_iota(jnp.int32, a.shape, 1)
    idx = lax.rem(2 * lane, half)
    low = lane < half // 2
    return jnp.concatenate(
        [jnp.where(low, lane_gather(a, idx + i), lane_gather(b, idx + i)) for i in range(2)], axis=1
    )


def interleave(x):
    half = x.shape[1] // 2
    even, odd = x[:, :half], x[:, half:]
    lane = lax.broadcasted_iota(jnp.int32, even.shape, 1)
    is_even = lax.rem(lane, 2) == 0
    idx = lane // 2
    return jnp.concatenate(
        [
            jnp.where(is_even, lane_gather(even, idx + h * (half // 2)), lane_gather(odd, idx + h * (half // 2)))
            for h in range(2)
        ],
        axis=1,
    )


def lay(nat, field):
    half = nat.shape[2]
    for h in range(2):
        nat[h] = field[:, h * half : (h + 1) * half]


def member_kernel(
    owner_rows, rb, unroll, q_ref, flow_ref, spread_ref, col_ref, var_ref, out_ref, hx_ref, coef, flow, buf_q, buf_a, buf_b, nat, sums
):
    v = pl.program_id(0)
    many = q_ref.shape[0]
    nv = sums.shape[1]
    nx, ny = q_ref.shape[2:]
    half = ny // 2
    t_rows = nx // SUB

    @pl.when(v == 0)
    def _():
        for c in range(2):
            lay(nat, flow_ref[c])

            def fill(t, _, c=c):
                flow[c, t] = 0.5 * strided(nat, t, t_rows)
                return 0

            lax.fori_loop(0, t_rows, fill, 0, unroll=8)

    lay(nat, spread_ref[0])

    def fill(t, _):
        store_coefs(coef, pl.ds(t + 1, 1), strided(nat, t, t_rows)[None], flow[0, pl.ds(t, 1)], flow[1, pl.ds(t, 1)])
        return 0

    lax.fori_loop(0, t_rows, fill, 0, unroll=8)
    for j in range(many):
        lay(nat, q_ref[j, 0])

        def fill(t, _, j=j):
            buf_q[t + 1, j * SUB : (j + 1) * SUB] = strided(nat, t, t_rows)
            return 0

        lax.fori_loop(0, t_rows, fill, 0, unroll=8)

    def wrap(buf):
        for j in range(many):
            s = slice(j * SUB, (j + 1) * SUB)
            buf[0, s] = pltpu.roll(buf[t_rows, s], 1, 0)
            buf[t_rows + 1, s] = pltpu.roll(buf[1, s], SUB - 1, 0)

    for step in range(STEPS):
        wrap(buf_q)
        stencil(buf_q, None, coef, 0, 1, t_rows + 1, rb, unroll, buf_a)
        wrap(buf_a)
        stencil(buf_a, buf_q, coef, 5, 1, t_rows + 1, rb, unroll, buf_b)
        wrap(buf_b)
        stencil(buf_b, buf_q, coef, 10, 1, t_rows + 1, rb, unroll, buf_q)

    height = out_ref.shape[3]
    per = t_rows // BLOCK * SUB
    for j in range(many):
        s = slice(j * SUB, (j + 1) * SUB)

        def put(t, _, s=s):
            for h in range(2):
                nat[h, pl.ds(t, SUB, stride=t_rows), :] = buf_q[t + 1, s, h * half : (h + 1) * half]
            return 0

        lax.fori_loop(0, t_rows, put, 0, unroll=8)
        for g, r in enumerate(owner_rows):
            for h in range(2):
                out_ref[g, 0, j, :, h * half : (h + 1) * half] = nat[h, r * height : (r + 1) * height, :]
        x = buf_q[1 : t_rows + 1, s].reshape(t_rows // BLOCK, BLOCK, SUB, ny)
        sums[j, v] = ((x[:, 0] + x[:, 1]) + (x[:, 2] + x[:, 3])).reshape(per, ny)

    @pl.when(v == nv - 1)
    def _():
        lanes = hx_ref.shape[2]
        column = lax.rem(lax.broadcasted_iota(jnp.int32, (ny, lanes), 0), half) // (BLOCK // 2)
        pool = (column == lax.broadcasted_iota(jnp.int32, (ny, lanes), 1)).astype(F32)
        pooled = exact_dot(sums[...].reshape(many * nv * per, ny), pool) * (1.0 / (BLOCK * BLOCK))
        for j in range(many):
            total = jnp.zeros((per, lanes), F32)
            for w in range(nv):
                at = (j * nv + w) * per
                chosen = lane_gather(pooled[at : at + per], col_ref[...])
                total = total + jnp.where(var_ref[...] == w, chosen, 0.0)
            hx_ref[j] = total


def member_forecast(first, many, ensemble, flow, spread, col, var, owner_rows):
    _, nv, nx, ny = ensemble.shape
    groups = len(owner_rows)
    height, t_rows = nx // groups, nx // SUB
    rb, unroll = (16, 2) if many == 1 else (8, 4)
    part = ensemble if many == ensemble.shape[0] else lax.slice_in_dim(ensemble, first, first + many, axis=0)
    return pl.pallas_call(
        functools.partial(member_kernel, owner_rows, rb, unroll),
        grid=(nv,),
        in_specs=[
            pl.BlockSpec((many, 1, nx, ny), lambda v: (0, v, 0, 0)),
            pl.BlockSpec((2, nx, ny), lambda v: (0, 0, 0)),
            pl.BlockSpec((1, nx, ny), lambda v: (v, 0, 0)),
            pl.BlockSpec(col.shape, lambda v: (0, 0)),
            pl.BlockSpec(var.shape, lambda v: (0, 0)),
        ],
        out_specs=[
            pl.BlockSpec((groups, 1, many, height, ny), lambda v: (0, v, 0, 0, 0)),
            pl.BlockSpec((many,) + col.shape, lambda v: (0, 0, 0)),
        ],
        out_shape=[
            jax.ShapeDtypeStruct((groups, nv, many, height, ny), F32),
            jax.ShapeDtypeStruct((many,) + col.shape, F32),
        ],
        scratch_shapes=[
            pltpu.VMEM((15, t_rows + 2, SUB, ny), F32),
            pltpu.VMEM((2, t_rows, SUB, ny), F32),
        ]
        + [pltpu.VMEM((t_rows + 2, many * SUB, ny), F32)] * 3
        + [pltpu.VMEM((2, nx, ny // 2), F32), pltpu.VMEM((many, nv, nx // BLOCK, ny), F32)],
        name=f"member_forecast_{many}",
    )(part, flow, spread, col, var)


def group_kernel(rb, unroll, x_ref, lo_ref, hi_ref, raw_ref, pick_ref, out_ref, hx_ref, coef, buf_q, buf_a, buf_b):
    height, _, ny = x_ref.shape
    halo = lo_ref.shape[0]
    total = height + 2 * halo

    @pl.when(pl.program_id(0) == 0)
    def _():
        def fill(i, _):
            rows = pl.ds(i, 1)
            store_coefs(coef, rows, raw_ref[0, rows], raw_ref[1, rows], raw_ref[2, rows])
            return 0

        lax.fori_loop(0, total, fill, 0, unroll=2)

    buf_q[:halo] = lo_ref[...]
    buf_q[halo : halo + height] = x_ref[...]
    buf_q[halo + height : total] = hi_ref[...]
    for step in range(STEPS):
        e = 3 * step
        stencil(buf_q, None, coef, 0, e + 1, total - e - 1, rb, unroll, buf_a)
        stencil(buf_a, buf_q, coef, 5, e + 2, total - e - 2, rb, unroll, buf_b)
        stencil(buf_b, buf_q, coef, 10, e + 3, total - e - 3, rb, unroll, buf_q)

    out_ref[...] = buf_q[halo : halo + height]
    per = pick_ref.shape[2]
    for b in range(height // BLOCK):
        at = halo + BLOCK * b
        rows_sum = (buf_q[at] + buf_q[at + 1]) + (buf_q[at + 2] + buf_q[at + 3])
        hi, mid, lo = thirds(rows_sum)
        pick = pick_ref[b]
        hx_ref[:, b * per : (b + 1) * per] = bdot(hi, pick) + (bdot(mid, pick) + bdot(lo, pick))


def group_forecast(first, mt, x, lo, hi, raw, pick):
    height, _, ny = x.shape
    halo, many = lo.shape[:2]
    total = height + 2 * halo
    width = pick.shape[0] * pick.shape[2]
    rb, unroll = 2, 4
    skip = first * (many // mt)
    return pl.pallas_call(
        functools.partial(group_kernel, rb, unroll),
        grid=(many // mt,),
        in_specs=[
            pl.BlockSpec((height, mt, ny), lambda i: (0, i + skip, 0)),
            pl.BlockSpec((halo, mt, ny), lambda i: (0, i, 0)),
            pl.BlockSpec((halo, mt, ny), lambda i: (0, i, 0)),
            pl.BlockSpec(raw.shape, lambda i: (0, 0, 0, 0)),
            pl.BlockSpec(pick.shape, lambda i: (0, 0, 0)),
        ],
        out_specs=[
            pl.BlockSpec((height, mt, ny), lambda i: (0, i, 0)),
            pl.BlockSpec((mt, width), lambda i: (i, 0)),
        ],
        out_shape=[
            jax.ShapeDtypeStruct((height, many, ny), F32),
            jax.ShapeDtypeStruct((many, width), F32),
        ],
        scratch_shapes=[pltpu.VMEM((15, total + rb * unroll, SUB, ny), F32)]
        + [pltpu.VMEM((total + rb * unroll, mt, ny), F32)] * 3,
        name="group_forecast",
    )(x, lo, hi, raw, pick)


def select_kernel(base_ref, chosen_ref, *refs):
    blocks, out_ref = refs[:-1], refs[-1]
    width = blocks[0].shape[2]
    count, _, slots = chosen_ref.shape
    chosen = jnp.concatenate([chosen_ref[p] for p in range(count)], axis=1)
    row = lax.broadcasted_iota(jnp.int32, (width, count * slots), 0)

    def part(block, base):
        pick = (row + base == chosen).astype(F32).astype(BF16)
        hi, mid, lo = thirds(block)
        return bdot(hi, pick) + (bdot(mid, pick) + bdot(lo, pick))

    if len(blocks) == 1:
        only = blocks[0]
        out_ref[...] = lax.fori_loop(
            0,
            only.shape[0],
            lambda b, acc: acc + part(only[b], base_ref[b]),
            jnp.zeros(out_ref.shape, F32),
        )
    else:
        total = part(blocks[0][0], base_ref[0])
        for b in range(1, len(blocks)):
            total = total + part(blocks[b][0], base_ref[b])
        out_ref[...] = total


def select(base, chosen, blocks):
    members = blocks[0].shape[1]
    return pl.pallas_call(
        select_kernel,
        in_specs=[pl.BlockSpec(memory_space=pltpu.SMEM)]
        + [pl.BlockSpec(memory_space=pltpu.VMEM)] * (1 + len(blocks)),
        out_specs=pl.BlockSpec(memory_space=pltpu.VMEM),
        out_shape=jax.ShapeDtypeStruct((members, chosen.shape[0] * chosen.shape[2]), F32),
        name="select",
    )(base, chosen, *blocks)


def transform_kernel(hx_ref, weight_ref, value_ref, out_ref):
    members = hx_ref.shape[0]
    count, _, slots = weight_ref.shape
    eye = (
        lax.broadcasted_iota(jnp.int32, (members, members), 0)
        == lax.broadcasted_iota(jnp.int32, (members, members), 1)
    ).astype(F32)
    scale = 1.0 / (members - 1)
    roots, drives, norms = [], [], []
    for p in range(count):
        part = hx_ref[:, p * slots : (p + 1) * slots]
        mean = jnp.mean(part, axis=0, keepdims=True)
        y = part - mean
        w = weight_ref[p]
        gram = lax.dot_general(
            y * w, y, (((1,), (1,)), ((), ())), precision=lax.Precision.HIGHEST, preferred_element_type=F32
        )
        system = eye + gram * scale
        norm = jnp.sqrt(jnp.sum(system * system, keepdims=True))
        roots.append(system / norm)
        norms.append(norm)
        drive = jnp.sum(y * (w * (value_ref[p] - mean)), axis=1, keepdims=True) * scale
        drives.append(jnp.broadcast_to(drive, (members, members)))
    inverses = [None] * count
    for sweep in range(NS_ITERS):
        for p in range(count):
            s = halves(roots[p])
            if sweep == 0:
                newton = 1.5 * eye - 0.5 * roots[p]
                inverses[p] = newton
                n = halves(newton)
            else:
                z = halves(inverses[p])
                newton = 1.5 * eye - 0.5 * dot3(z, s)
                n = halves(newton)
                inverses[p] = dot3(n, z)
            if sweep < NS_ITERS - 1:
                roots[p] = dot3(s, n)
    for p in range(count):
        z = halves(inverses[p])
        mean_w = dot3(z, halves(dot3(z, halves(drives[p])))) / norms[p]
        out_ref[p] = inverses[p] / jnp.sqrt(norms[p]) + mean_w


def transforms(hx, weight, value):
    members = hx.shape[0]
    return pl.pallas_call(
        transform_kernel,
        in_specs=[pl.BlockSpec(memory_space=pltpu.VMEM)] * 3,
        out_specs=pl.BlockSpec(memory_space=pltpu.VMEM),
        out_shape=jax.ShapeDtypeStruct((weight.shape[0], members, members), F32),
        name="transforms",
    )(hx, weight, value)


def mix(transform, x):
    mean = jnp.mean(x, axis=0, keepdims=True)
    return mean + dot3(halves(transform.T), halves(x - mean))


def first_analysis_kernel(count, nparts, chunks, q_ref, *refs):
    gs, parts, outs = refs[: len(refs) - nparts - 1 - 2 * chunks], refs[-nparts - 1 - 2 * chunks : -1 - 2 * chunks], refs[-1 - 2 * chunks :]
    out_ref, sends = outs[0], outs[1:]
    tile = pl.program_id(0)
    ny = out_ref.shape[2]
    for p in range(SUB // PR):
        patch = tile * (SUB // PR) + p
        g = gs[0][lax.bitwise_xor(patch // count, q_ref[0]), lax.rem(patch, count)]
        x = jnp.concatenate(
            [
                jnp.concatenate(
                    [part[:, j, PR * p + i, :] for part in parts for j in range(part.shape[1])], axis=0
                )
                for i in range(PR)
            ],
            axis=1,
        )
        y = mix(g, x)
        for i in range(PR):
            out_ref[PR * p + i] = y[:, i * ny : (i + 1) * ny]
    if chunks:
        halo, many = sends[0].shape[:2]
        height = SUB * pl.num_programs(0)
        tiles = -(-halo // SUB)
        for c in range(chunks):
            lo, hi = sends[2 * c], sends[2 * c + 1]
            members = slice(c * many, (c + 1) * many)
            for k in range(tiles):

                @pl.when(tile == k)
                def _():
                    rows = min(SUB, halo - SUB * k)
                    hi[SUB * k : SUB * k + rows] = out_ref[:rows, members]

                @pl.when(tile == pl.num_programs(0) - 1 - k)
                def _():
                    rows = min(SUB, halo - SUB * k)
                    lo[halo - SUB * k - rows : halo - SUB * k] = out_ref[SUB - rows :, members]


def first_analysis(q, g, parts, chunks):
    n, _, height, ny = parts[0].shape
    members = n * sum(part.shape[1] for part in parts)
    if HALO > height:
        chunks = 0
    sends = [(HALO, members // chunks, ny)] * (2 * chunks) if chunks else []
    return pl.pallas_call(
        functools.partial(first_analysis_kernel, g.shape[1], len(parts), chunks),
        grid=(height // SUB,),
        in_specs=[
            pl.BlockSpec(memory_space=pltpu.SMEM),
            pl.BlockSpec(g.shape, lambda i: (0, 0, 0, 0)),
        ]
        + [pl.BlockSpec((n, part.shape[1], SUB, ny), lambda i: (0, 0, i, 0)) for part in parts],
        out_specs=[pl.BlockSpec((SUB, members, ny), lambda i: (i, 0, 0))]
        + [pl.BlockSpec(s, lambda i: (0, 0, 0)) for s in sends],
        out_shape=[jax.ShapeDtypeStruct((height, members, ny), F32)]
        + [jax.ShapeDtypeStruct(s, F32) for s in sends],
        name="first_analysis",
    )(q, g, *parts)


def last_analysis_kernel(nparts, at_ref, g_ref, *refs):
    xs, out_ref = refs[:nparts], refs[nparts]
    count = g_ref.shape[1]
    n, _, mine, rows, ny = out_ref.shape
    for p in range(rows // PR):
        g = g_ref[0, p]
        x = jnp.concatenate(
            [jnp.concatenate([part[PR * p + i] for part in xs], axis=0) for i in range(PR)], axis=1
        )
        y = mix(g, x)
        for i in range(PR):
            for j in range(mine):
                out_ref[:, 0, j, PR * p + i, :] = y[j * n : (j + 1) * n, i * ny : (i + 1) * ny]


def last_analysis(at, g, xs, n):
    quarters, count, members, _ = g.shape
    ny = xs[0].shape[2]
    rows = count * PR
    mine = members // n
    return pl.pallas_call(
        functools.partial(last_analysis_kernel, len(xs)),
        grid_spec=pltpu.PrefetchScalarGridSpec(
            num_scalar_prefetch=1,
            grid=(quarters,),
            in_specs=[pl.BlockSpec((1, count, members, members), lambda i, at: (i, 0, 0, 0))]
            + [pl.BlockSpec((rows, part.shape[1], ny), lambda i, at: (at[i], 0, 0)) for part in xs],
            out_specs=pl.BlockSpec((n, 1, mine, rows, ny), lambda i, at: (0, i, 0, 0, 0)),
        ),
        out_shape=jax.ShapeDtypeStruct((n, quarters, mine, rows, ny), F32),
        name="last_analysis",
    )(at, g, *xs)


def assemble_kernel(nv, a_ref, b_ref, out_ref):
    mine, _, height, ny = out_ref.shape
    rows = height // nv
    for v in range(nv):
        for c in range(nv):
            src = a_ref[v, 0] if c == 0 else b_ref[v, c - 1]
            at = (v ^ c) * rows
            whole = interleave(src.reshape(mine * rows, ny)).reshape(mine, rows, ny) if rows % SUB == 0 else None
            for j in range(mine):
                out_ref[j, v, at : at + rows, :] = interleave(src[j]) if whole is None else whole[j]


def assemble(nv, a, b, nx):
    n, _, mine, rows, ny = a.shape
    groups = n // nv
    height = nx // groups
    spot = lambda g: lax.select(g % 2 == 0, g // 2, groups - 1 - g // 2) if groups > 1 else g
    return pl.pallas_call(
        functools.partial(assemble_kernel, nv),
        grid=(groups,),
        in_specs=[
            pl.BlockSpec((nv, 1, mine, rows, ny), lambda g: (g, 0, 0, 0, 0)),
            pl.BlockSpec((nv, nv - 1, mine, rows, ny), lambda g: (g, 0, 0, 0, 0)),
        ],
        out_specs=pl.BlockSpec((mine, nv, height, ny), lambda g: (0, 0, spot(g), 0)),
        out_shape=jax.ShapeDtypeStruct((mine, nv, nx, ny), F32),
        name="assemble",
    )(a, b)


def local(n, ensemble, flow_speed, spreading, obs_values, obs_var, obs_block, readers, counts):
    mine, nv, nx, ny = ensemble.shape
    members = mine * n
    nobs = obs_var.shape[0]
    patches, slots = readers.shape
    groups = n // nv
    height = nx // groups
    count = patches // n
    width = nobs // n
    nbr, nbc = nx // BLOCK, ny // BLOCK
    per_row = nobs // nbr
    half = ny // 2

    place = [2 * r if 2 * r < groups else 2 * (groups - 1 - r) + 1 for r in range(groups)]
    owner_rows = [place.index(g) for g in range(groups)]
    device = lambda s: nv * place[(s // nv) % groups] + s % nv

    me = lax.axis_index("dev")
    q = lax.rem(me, nv)
    g = me // nv
    r = jnp.where(g % 2 == 0, g // 2, groups - 1 - g // 2) if groups > 1 else g * 0
    spot = r * nv + q
    q_ref = q.reshape(1).astype(jnp.int32)

    def send(x, hop):
        return lax.ppermute(x, "dev", [(device(s), device((s + hop) % n)) for s in range(n)])

    def swap(x, c):
        return lax.ppermute(x, "dev", [(d, d ^ c) for d in range(n)])

    obs_col = (obs_block % nbc).reshape(nbr, per_row)
    obs_v = (obs_block // (nbr * nbc)).reshape(nbr, per_row)
    lanes = max(128, nbc)

    def table(a):
        a = a.reshape(SUB, nbr // SUB, per_row).transpose(1, 0, 2).reshape(nbr, per_row)
        return jnp.pad(a, ((0, 0), (0, lanes - per_row)))

    col_table, var_table = table(obs_col), table(obs_v)

    forecast = lambda first, many: member_forecast(
        first, many, ensemble, flow_speed, spreading, col_table, var_table, owner_rows
    )
    send_all = lambda x: lax.all_to_all(x, "dev", 0, 0, tiled=True)
    cuts = [(0, 1), (1, mine - 1)] if mine > 1 else [(0, 1)]
    parts, observed = [], []
    for first, many in cuts:
        fields, hx = forecast(first, many)
        parts.append(fields.reshape(n, many, height, ny))
        observed.append(hx)
    arrived = [send_all(parts[0])]
    observed = jnp.concatenate(observed, 0)[:, :, :per_row]
    observed = observed.reshape(mine, nbr // SUB, SUB, per_row).transpose(0, 2, 1, 3).reshape(mine, groups, nv, width)
    observed = jnp.stack([observed[:, r0] for r0 in owner_rows], 0).transpose(0, 2, 1, 3).reshape(n, mine, width)
    observed = send_all(observed)
    if mine > 1:
        rest, observed = lax.optimization_barrier((parts[1], observed))
        arrived.append(send_all(rest))
    hx = observed.transpose(1, 0, 2).reshape(members, width)

    first = spot * count
    chosen = lax.dynamic_slice_in_dim(readers, first, count, 0)
    my_counts = lax.dynamic_slice_in_dim(counts, first, count, 0)
    patch_index = first + jnp.arange(count, dtype=jnp.int32)
    obs_row = (chosen * nbr // nobs).astype(F32) * BLOCK + 0.5 * (BLOCK - 1)
    patch_row = patch_index.astype(F32) * PR + 0.5 * (PR - 1)
    gap = jnp.abs(obs_row - patch_row[:, None])
    distance = jnp.minimum(gap, nx - gap)
    taper = jnp.exp(-0.5 * (distance / TAPER_ROWS) ** 2)
    listed = jnp.arange(slots, dtype=jnp.int32) < my_counts[:, None]
    weight = jnp.where(listed, taper / obs_var[chosen], 0.0)[:, None, :]
    values = obs_values[:, chosen][:, :, None, :]
    chosen = chosen[:, None, :]

    reach = -(-NEAR * per_row // width) + (1 if width < per_row else 0)
    reach = min(reach, (n - 1) // 2)
    owner = jnp.arange(patches, dtype=jnp.int32)[:, None] // count
    away = lax.rem(readers // width - owner + (n + reach), n)
    read = jnp.arange(slots, dtype=jnp.int32) < counts[:, None]
    near = jnp.all((away <= 2 * reach) | ~read)

    start = r * height - HALO + nx
    take = lambda a: lax.dynamic_slice_in_dim(jnp.concatenate([a, a, a], -2), start, height + 2 * HALO, a.ndim - 2)
    my_spread = take(lax.dynamic_index_in_dim(spreading, q, 0, keepdims=True))
    raw = jnp.concatenate([my_spread, 0.5 * take(flow_speed)], 0)
    raw = raw.reshape(raw.shape[:2] + (half, 2)).transpose(0, 1, 3, 2).reshape(raw.shape)
    raw = jnp.broadcast_to(raw[:, :, None, :], raw.shape[:2] + (SUB, ny))
    block_rows = height // BLOCK
    group_col = lax.dynamic_slice_in_dim(obs_col, r * block_rows, block_rows, 0)
    group_var = lax.dynamic_slice_in_dim(obs_v, r * block_rows, block_rows, 0)
    column = (jnp.arange(ny, dtype=jnp.int32) % half) // (BLOCK // 2)
    pick = jnp.where(
        (column[None, :, None] == group_col[:, None, :]) & (group_var[:, None, :] == q),
        1.0 / (BLOCK * BLOCK),
        0.0,
    ).astype(BF16)

    def solve(cycle, hx):
        shifts = list(range(-reach, reach + 1))
        blocks = [hx if o == 0 else send(hx, -o) for o in shifts]
        base = (spot + jnp.array(shifts, jnp.int32) + n) % n * width

        def close(hx, *blocks):
            return select(base, chosen, [b[None] for b in blocks])

        def far(hx, *blocks):
            every = lax.all_to_all(jnp.broadcast_to(hx[None], (n,) + hx.shape), "dev", 0, 0, tiled=True)
            owner = [(owner_rows[d // nv] * nv + d % nv) * width for d in range(n)]
            return select(jnp.array(owner, jnp.int32), chosen, [every])

        picked = lax.cond(near, close, far, hx, *blocks)
        return transforms(picked, weight, values[cycle])

    own = solve(0, hx)
    every = jnp.stack([own] + [swap(own, c) for c in range(1, nv)])
    every, raw, pick, values = lax.optimization_barrier((every, raw, pick, values))
    chunks = 2 if HALO <= height else 1
    state, *sends = first_analysis(q_ref, every, arrived, chunks)

    if not sends:
        sends = [state, state]
    advanced, partial = [], []
    for c in range(chunks):
        lo, hi = [], []
        left, hop = HALO, 1
        while left > 0:
            rows_k = min(left, height)
            down, up = sends[2 * c], sends[2 * c + 1]
            lo.insert(0, send(down[down.shape[0] - rows_k :], hop * nv))
            hi.append(send(up[:rows_k], -hop * nv))
            left -= rows_k
            hop += 1
        lo = lo[0] if len(lo) == 1 else jnp.concatenate(lo, 0)
        hi = hi[0] if len(hi) == 1 else jnp.concatenate(hi, 0)
        out, hx = group_forecast(c, min(64, lo.shape[1]), state, lo, hi, raw, pick)
        advanced.append(out)
        partial.append(hx)
    partial = (jnp.concatenate(partial, 0) if chunks > 1 else partial[0]).reshape(members, nv, width)
    pieces = [lax.dynamic_index_in_dim(partial, q, 1, keepdims=False)]
    for c in range(1, nv):
        other = lax.dynamic_index_in_dim(partial, lax.bitwise_xor(q, c), 1, keepdims=False)
        pieces.append(swap(other, c))
    hx = functools.reduce(lambda a, b: a + b, pieces)

    own = solve(1, hx)
    others = [swap(own, c) for c in range(1, nv)]
    front = last_analysis(q_ref, own[None], advanced, n)
    at = lax.bitwise_xor(q, jnp.arange(1, nv, dtype=jnp.int32))
    back = last_analysis(at, jnp.stack(others), advanced, n)
    return assemble(nv, send_all(front), send_all(back), nx)


def solution(mesh):
    n = mesh.shape["dev"]
    return jax.shard_map(
        functools.partial(local, n),
        mesh=mesh,
        in_specs=(P("dev", None, None, None), P(), P(), P(), P(), P(), P(), P()),
        out_specs=P("dev", None, None, None),
        check_vma=False,
    )
```

time: 746 us -> 395 us (0.53)
  Pallas kernels: 316 us -> 121 us
  waiting for transfers between devices: 238 us -> 93 us
  local copies, waits for them, and re-layouts: 41.1 us -> 30.8 us
    pallas_call x7 -> x10, Pallas kernels: 276 us -> 101 us  [the longest x2 42.3 us: member_forecast(): pl.pallas_call(functools.partial(member_kernel, owner_rows, rb, unroll),...]
    all_to_all x7 -> x3, waiting for transfers between devices: 184 us -> 24 us  [local(): send_all = lambda x: lax.all_to_all(x, 'dev', 0, 0, tiled=True)]
    pallas_call x2, Pallas kernels: 40 us -> 20.2 us  [transforms(): pl.pallas_call(transform_kernel, in_specs=[pl.BlockSpec(memory_space=pltp...]
    ppermute x11 -> x21, waiting for transfers between devices: 54 us -> 69 us  [the longest x9 42.9 us: swap(): return lax.ppermute(x, 'dev', [(d, d ^ c) for d in range(n)])]
    all_to_all x7 -> x3, starting transfers between devices: 26.5 us -> 14 us  [local(): send_all = lambda x: lax.all_to_all(x, 'dev', 0, 0, tiled=True)]
    ppermute x11 -> x21, starting transfers between devices: 7.95 us -> 15.2 us  [the longest x12 9.17 us: send(): lax.ppermute(x, 'dev', [(device(s), device((s + hop) % n)) for s in range...]
    all_to_all x4 -> x2, blocking collectives: 103 us -> 105 us  [local(): send_all = lambda x: lax.all_to_all(x, 'dev', 0, 0, tiled=True)]
  transfers between devices with their start and end apart: 18 -> 24, of which waited for: 14 -> 17; matrix products, arithmetic and copies ran while one was open for 4% -> 7% of each run, Pallas kernels for 3% -> 8%
where the time goes in v2:
time: 395 us; the launch traced here: 393 us
  Pallas kernels  121 us (31%)
  blocking collectives  105 us (27%)
  waiting for transfers between devices  93 us (24%)
  local copies, waits for them, and re-layouts  30.8 us (8%)
  starting transfers between devices  29.2 us (7%)
  other arithmetic  12.8 us (3%)
    all_to_all x2, blocking collectives, local(): send_all = lambda x: lax.all_to_all(x, 'dev', 0, 0, tiled=True)  105 us
    ppermute x9, waiting for transfers between devices, swap(): return lax.ppermute(x, 'dev', [(d, d ^ c) for d in range(n)])  42.9 us
    pallas_call x2, Pallas kernels, member_forecast(): pl.pallas_call(functools.partial(member_kernel, owner_rows, rb, unroll),...  42.3 us
    pallas_call x2, Pallas kernels, group_forecast(): pl.pallas_call(functools.partial(group_kernel, rb, unroll), grid=(many //...  30.4 us
    ppermute x12, waiting for transfers between devices, send(): lax.ppermute(x, 'dev', [(device(s), device((s + hop) % n)) for s in range...  26.2 us
    all_to_all x3, waiting for transfers between devices, local(): send_all = lambda x: lax.all_to_all(x, 'dev', 0, 0, tiled=True)  24 us
    pallas_call x2, Pallas kernels, transforms(): pl.pallas_call(transform_kernel, in_specs=[pl.BlockSpec(memory_space=pltp...  20.2 us
    all_to_all x3, starting transfers between devices, local(): send_all = lambda x: lax.all_to_all(x, 'dev', 0, 0, tiled=True)  14 us
  transfers between devices with their start and end apart: 24, of which 17 were waited for; matrix products, arithmetic and copies ran while one was open for 7% of the time, Pallas kernels for 8%

profile of v2, /device:TPU:0, one launch (start us, length us, event | category | flops | bytes accessed | tf_op | source)
XLA Modules:
  0.0 393.3 jit_solution(2446451224550442083)
XLA Ops:
  0.0 2.4 slice.41.q_ref
  2.4 3.8 slice.40.q_ref
  7.5 14.0 %member_forecast_1.1 = (f32[8,4,1,32,256]{4,3,2,1,0:T(8,128)}, f32[1,64,128]{2,1,0:T(8,128)}) custom-call(f32[1,4,256,256]{3,2,1,0:T(8,128)} %slice.41.q_ref, f32[2,256,256]{2,1,0:T(8,128)} %flow_ref.3, f32[4,256,256]{2,1,0:T(8,128)} %spread_ref.3, s32[64,128]{1,0:T(8,128)} %pad.7.col_ref, s32[64,128]{1,0:T(8,128)} %pad.8.var_ref), custom_call_target="tpu_custom_call" | custom-call | tf_op jit(solution)/shard_map/member_forecast_1/pallas_call | solution.py:208
  21.6 28.2 %member_forecast_3.1 = (f32[8,4,3,32,256]{4,3,2,1,0:T(8,128)}, f32[3,64,128]{2,1,0:T(8,128)}) custom-call(f32[3,4,256,256]{3,2,1,0:T(8,128)} %slice.40.q_ref, f32[2,256,256]{2,1,0:T(8,128)} %flow_ref.3, f32[4,256,256]{2,1,0:T(8,128)} %spread_ref.3, s32[64,128]{1,0:T(8,128)} %pad.7.col_ref, s32[64,128]{1,0:T(8,128)} %pad.8.var_ref), custom_call_target="tpu_custom_call" | custom-call | tf_op jit(solution)/shard_map/member_forecast_3/pallas_call | solution.py:208
  51.7 7.3 %all-to-all-start.2 = ((f32[32,4,128]{2,1,0:T(4,128)}), f32[32,4,128]{2,1,0:T(4,128)S(1)}, u32[]{:S(2)}, u32[]{:S(2)}) async-start(f32[32,4,128]{2,1,0:T(4,128)} %copy.84), calls=%async_computation.2 | async-start | bytes 131072 | tf_op jit(solution)/shard_map/all_to_all | solution.py:568
  60.6 5.9 %all-to-all-done.2 = f32[32,4,128]{2,1,0:T(4,128)S(1)} async-done(((f32[32,4,128]{2,1,0:T(4,128)}), f32[32,4,128]{2,1,0:T(4,128)S(1)}, u32[]{:S(2)}, u32[]{:S(2)}) %all-to-all-start.2) | async-done | bytes 65568 | tf_op jit(solution)/shard_map/all_to_all | solution.py:568
  69.0 2.2 collective-permute-done.3
  71.3 1.5 collective-permute-done.2
  72.8 2.3 collective-permute-done.1
  76.1 1.8 conditional.2
  76.6 1.3 select.72
  77.9 28.6 %all_to_all.35.refs_1_ = f32[32,1,32,256]{3,2,1,0:T(8,128)} all-to-all(f32[32,1,32,256]{3,2,1,0:T(8,128)S(1)} %bitcast.115), channel_id=1, replica_groups=mesh['dev'=32] {'dev'}, dimensions={0} | all-to-all | bytes 2097152 | tf_op jit(solution)/shard_map/all_to_all | solution.py:568
  106.5 3.7 all-to-all-start.4
  110.5 2.7 copy.86
  113.2 3.1 gather_fusion
  116.3 3.2 gather_fusion.1
  125.8 10.1 %transforms.2 = f32[4,128,128]{2,1,0:T(8,128)} custom-call(f32[128,512]{1,0:T(8,128)S(1)} %get-tuple-element.201.hx_ref, f32[4,1,128]{2,1,0:T(1,128)} %bitcast.153, f32[4,1,128]{2,1,0:T(1,128)} %bitcast.158), custom_call_target="tpu_custom_call" | custom-call | tf_op jit(solution)/shard_map/transforms/pallas_call | solution.py:385
  135.9 1.3 collective-permute-start.6
  141.3 1.8 select_convert_fusion.pick_ref
  143.1 11.0 %collective-permute-done.6 = f32[4,128,128]{2,1,0:T(8,128)} collective-permute-done((f32[4,128,128]{2,1,0:T(8,128)}, f32[4,128,128]{2,1,0:T(8,128)}, u32[]{:S(2)}, u32[]{:S(2)}) %collective-permute-start.6) | collective-permute-done | bytes 262176 | tf_op jit(solution)/shard_map/ppermute | solution.py:553
  154.0 5.9 %collective-permute-done.5 = f32[4,128,128]{2,1,0:T(8,128)} collective-permute-done((f32[4,128,128]{2,1,0:T(8,128)}, f32[4,128,128]{2,1,0:T(8,128)}, u32[]{:S(2)}, u32[]{:S(2)}) %collective-permute-start.5) | collective-permute-done | bytes 262176 | tf_op jit(solution)/shard_map/ppermute | solution.py:553
  159.9 2.3 pad_maximum_fusion.refs_0_
  163.4 18.1 %all-to-all-done.4.refs_2_ = f32[32,3,32,256]{3,2,1,0:T(8,128)S(1)} async-done(((f32[32,3,32,256]{3,2,1,0:T(8,128)}), f32[32,3,32,256]{3,2,1,0:T(8,128)S(1)}, u32[]{:S(2)}, u32[]{:S(2)}) %all-to-all-start.4) | async-done | bytes 3145760 | tf_op jit(solution)/shard_map/all_to_all | solution.py:568
  181.5 1.6 copy-done.1
  183.1 8.2 %first_analysis.1 = (f32[32,128,256]{2,1,0:T(8,128)}, f32[9,64,256]{2,1,0:T(8,128)}, f32[9,64,256]{2,1,0:T(8,128)}, f32[9,64,256]{2,1,0:T(8,128)}, f32[9,64,256]{2,1,0:T(8,128)}) custom-call(s32[1]{0:T(128)} %bitcast.11.q_ref.at_ref, f32[4,4,128,128]{3,2,1,0:T(8,128)} %pad_maximum_fusion.refs_0_, f32[32,1,32,256]{3,2,1,0:T(8,128)} %all_to_all.35.refs_1_, ...), custom_call_target="tpu_custom_call" | custom-call | tf_op jit(solution)/shard_map/first_analysis/pallas_call | solution.py:445
  191.3 2.0 collective-permute-start.10
  193.3 2.0 collective-permute-start.8
  195.3 12.4 %collective-permute-done.9.lo_ref = f32[9,64,256]{2,1,0:T(8,128)S(1)} collective-permute-done((f32[9,64,256]{2,1,0:T(8,128)}, f32[9,64,256]{2,1,0:T(8,128)S(1)}, u32[]{:S(2)}, u32[]{:S(2)}) %collective-permute-start.9) | collective-permute-done | bytes 589856 | tf_op jit(solution)/shard_map/ppermute | solution.py:550
  208.7 15.2 %group_forecast.3 = (f32[32,64,256]{2,1,0:T(8,128)}, f32[64,512]{1,0:T(8,128)}) custom-call(f32[32,128,256]{2,1,0:T(8,128)} %get-tuple-element.165.x_ref, f32[9,64,256]{2,1,0:T(8,128)} %copy-done.7, f32[9,64,256]{2,1,0:T(8,128)} %copy-done.8, f32[3,50,8,256]{3,2,1,0:T(8,128)} %broadcast_in_dim.89.raw_ref, bf16[8,256,64]{2,1,0:T(8,128)(2,1)} %select_convert_fusion.pick_ref), custom_call_target="tpu_custom_call" | custom-call | tf_op jit(solution)/shard_map/group_forecast/pallas_call | solution.py:276
  225.6 15.2 %group_forecast.2 = (f32[32,64,256]{2,1,0:T(8,128)}, f32[64,512]{1,0:T(8,128)}) custom-call(f32[32,128,256]{2,1,0:T(8,128)} %get-tuple-element.165.x_ref, f32[9,64,256]{2,1,0:T(8,128)} %copy-done.5, f32[9,64,256]{2,1,0:T(8,128)} %copy-done.6, f32[3,50,8,256]{3,2,1,0:T(8,128)} %broadcast_in_dim.89.raw_ref, bf16[8,256,64]{2,1,0:T(8,128)(2,1)} %select_convert_fusion.pick_ref), custom_call_target="tpu_custom_call" | custom-call | tf_op jit(solution)/shard_map/group_forecast/pallas_call | solution.py:276
  242.1 1.4 collective-permute-start.11
  244.3 2.1 collective-permute-done.13
  246.4 1.4 collective-permute-done.12
  247.8 2.1 collective-permute-start.17
  251.0 2.5 collective-permute-done.17
  253.4 1.4 collective-permute-done.16
  254.8 3.5 collective-permute-done.14
  258.3 2.1 conditional.3
  258.9 1.3 select.74
  260.5 10.1 %transforms.3 = f32[4,128,128]{2,1,0:T(8,128)} custom-call(f32[128,512]{1,0:T(8,128)S(1)} %get-tuple-element.202.hx_ref, f32[4,1,128]{2,1,0:T(1,128)} %bitcast.154, f32[4,1,128]{2,1,0:T(1,128)} %bitcast.157), custom_call_target="tpu_custom_call" | custom-call | tf_op jit(solution)/shard_map/transforms/pallas_call | solution.py:385
  270.6 3.2 last_analysis.2
  273.8 2.9 all-to-all-start.5
  276.7 1.6 collective-permute-start.20
  279.2 14.5 %collective-permute-done.20 = f32[4,128,128]{2,1,0:T(8,128)S(1)} collective-permute-done((f32[4,128,128]{2,1,0:T(8,128)S(1)}, f32[4,128,128]{2,1,0:T(8,128)S(1)}, u32[]{:S(2)}, u32[]{:S(2)}) %collective-permute-start.20) | collective-permute-done | bytes 262176 | tf_op jit(solution)/shard_map/ppermute | solution.py:553
  293.7 8.0 %collective-permute-done.19 = f32[4,128,128]{2,1,0:T(8,128)S(1)} collective-permute-done((f32[4,128,128]{2,1,0:T(8,128)S(1)}, f32[4,128,128]{2,1,0:T(8,128)S(1)}, u32[]{:S(2)}, u32[]{:S(2)}) %collective-permute-start.19) | collective-permute-done | bytes 262176 | tf_op jit(solution)/shard_map/ppermute | solution.py:553
  302.7 6.4 %last_analysis.3 = f32[32,3,4,8,256]{4,3,2,1,0:T(8,128)} custom-call(s32[3]{0:T(128)} %add_xor_fusion.at_ref, f32[3,4,128,128]{3,2,1,0:T(8,128)} %pad_maximum_fusion.1.g_ref, f32[32,64,256]{2,1,0:T(8,128)} %get-tuple-element.175.refs_0_, f32[32,64,256]{2,1,0:T(8,128)} %get-tuple-element.176.refs_1_), custom_call_target="tpu_custom_call" | custom-call | tf_op jit(solution)/shard_map/last_analysis/pallas_call | solution.py:481
  309.1 76.1 %all_to_all.36.b_ref = f32[32,3,4,8,256]{4,3,2,1,0:T(8,128)} all-to-all(f32[32,3,4,8,256]{4,3,2,1,0:T(8,128)} %last_analysis.3), channel_id=1, replica_groups=mesh['dev'=32] {'dev'}, dimensions={0} | all-to-all | bytes 6291456 | tf_op jit(solution)/shard_map/all_to_all | solution.py:568
  385.2 8.1 %assemble.1 = f32[4,4,256,256]{3,2,1,0:T(8,128)} custom-call(f32[32,1,4,8,256]{4,3,2,1,0:T(8,128)} %copy-done.2, f32[32,3,4,8,256]{4,3,2,1,0:T(8,128)} %all_to_all.36.b_ref), custom_call_target="tpu_custom_call" | custom-call | tf_op jit(solution)/shard_map/assemble/pallas_call | solution.py:512
  (142 shorter events, 28.0 us)
Async XLA Ops:
  0.0 113.2 %copy-start = (f32[4096]{0:T(1024)S(1)}, f32[4096]{0:T(1024)}, u32[]{:S(2)}) copy-start(f32[4096]{0:T(1024)} %param.20) | copy-start | bytes 49156
  2.4 3.8 copy-start.16
  21.6 28.3 %copy-start.13 = (f32[1,64,128]{2,1,0:T(8,128)S(1)}, f32[1,64,128]{2,1,0:T(8,128)}, u32[]{:S(2)}) copy-start(f32[1,64,128]{2,1,0:T(8,128)} %get-tuple-element.159) | copy-start | bytes 98308
  21.6 37.6 %copy-start.12 = (s32[128,128]{1,0:T(8,128)S(1)}, s32[128,128]{1,0:T(8,128)}, u32[]{:S(2)}) copy-start(s32[128,128]{1,0:T(8,128)} %param.22) | copy-start | bytes 196612
  21.6 37.6 %copy-start.29 = (s32[128]{0:T(128)S(1)}, s32[128]{0:T(128)}, u32[]{:S(2)}) copy-start(s32[128]{0:T(128)} %param.23) | copy-start | bytes 1540
  21.6 39.0 %copy-start.30 = (s32[5]{0:T(128)S(1)}, s32[5]{0:T(128)}, u32[]{:S(2)}) copy-start(s32[5]{0:T(128)} %constant.212.clone) | copy-start | bytes 64
  21.6 53.9 %copy-start.17 = (s32[32]{0:T(128)S(1)}, s32[32]{0:T(128)}, u32[]{:S(2)}) copy-start(s32[32]{0:T(128)} %constant.213.clone) | copy-start | bytes 388
  51.7 14.7 %all-to-all-start.2 = ((f32[32,4,128]{2,1,0:T(4,128)}), f32[32,4,128]{2,1,0:T(4,128)S(1)}, u32[]{:S(2)}, u32[]{:S(2)}) async-start(f32[32,4,128]{2,1,0:T(4,128)} %copy.84), calls=%async_computation.2 | async-start | bytes 131072 | tf_op jit(solution)/shard_map/all_to_all | solution.py:568
  60.6 15.0 %copy-start.19 = (s32[5]{0:T(128)}, s32[5]{0:T(128)S(1)}, u32[]{:S(2)}) copy-start(s32[5]{0:T(128)S(1)} %add_add_fusion.1) | copy-start | bytes 64
  66.5 4.8 %collective-permute-start.3 = (f32[128,128]{1,0:T(8,128)S(1)}, f32[128,128]{1,0:T(8,128)S(1)}, u32[]{:S(2)}, u32[]{:S(2)}) collective-permute-start(f32[128,128]{1,0:T(8,128)S(1)} %bitcast.118), channel_id=1, source_target_pairs={{0,6},{1,7},{2,0},{3,1},{8,2},{9,3},{10,8},{11,9},{16,10},{17,11},... | collective-permute-start | bytes 196616 | tf_op jit(solution)/shard_map/ppermute | solution.py:550
  67.2 5.6 %collective-permute-start.2 = (f32[128,128]{1,0:T(8,128)S(1)}, f32[128,128]{1,0:T(8,128)S(1)}, u32[]{:S(2)}, u32[]{:S(2)}) collective-permute-start(f32[128,128]{1,0:T(8,128)S(1)} %bitcast.119), channel_id=1, source_target_pairs={{0,7},{1,0},{2,1},{3,2},{8,3},{9,8},{10,9},{11,10},{16,11},{17,16}... | collective-permute-start | bytes 196616 | tf_op jit(solution)/shard_map/ppermute | solution.py:550
  67.9 7.2 %collective-permute-start.1 = (f32[128,128]{1,0:T(8,128)S(1)}, f32[128,128]{1,0:T(8,128)S(1)}, u32[]{:S(2)}, u32[]{:S(2)}) collective-permute-start(f32[128,128]{1,0:T(8,128)S(1)} %bitcast.120), channel_id=1, source_target_pairs={{0,1},{1,2},{2,3},{3,8},{8,9},{9,10},{10,11},{11,16},{16,17},{17,1... | collective-permute-start | bytes 196616 | tf_op jit(solution)/shard_map/ppermute | solution.py:550
  67.9 7.6 %collective-permute-start = (f32[128,128]{1,0:T(8,128)S(1)}, f32[128,128]{1,0:T(8,128)S(1)}, u32[]{:S(2)}, u32[]{:S(2)}) collective-permute-start(f32[128,128]{1,0:T(8,128)S(1)} %bitcast.121), channel_id=1, source_target_pairs={{0,2},{1,3},{2,8},{3,9},{8,10},{9,11},{10,16},{11,17},{16,18},{17,... | collective-permute-start | bytes 196616 | tf_op jit(solution)/shard_map/ppermute | solution.py:550
  69.0 56.1 %copy-start.10 = (s32[4,128]{1,0:T(4,128)}, s32[4,128]{1,0:T(4,128)S(1)}, u32[]{:S(2)}) copy-start(s32[4,128]{1,0:T(4,128)S(1)} %get-tuple-element.192) | copy-start | bytes 6148
  75.5 2.4 copy-start.4
  106.5 75.0 %all-to-all-start.4 = ((f32[32,3,32,256]{3,2,1,0:T(8,128)}), f32[32,3,32,256]{3,2,1,0:T(8,128)S(1)}, u32[]{:S(2)}, u32[]{:S(2)}) async-start(f32[32,3,32,256]{3,2,1,0:T(8,128)} %bitcast.112), calls=%async_computation.4 | async-start | bytes 6291456 | tf_op jit(solution)/shard_map/all_to_all | solution.py:568
  120.6 17.1 %copy-start.14 = (f32[4,128,2]{1,0,2:T(4,128)}, f32[4,128,2]{1,0,2:T(4,128)S(1)}, u32[]{:S(2)}) copy-start(f32[4,128,2]{1,0,2:T(4,128)S(1)} %copy.91) | copy-start | bytes 12292
  135.9 18.1 %collective-permute-start.6 = (f32[4,128,128]{2,1,0:T(8,128)}, f32[4,128,128]{2,1,0:T(8,128)}, u32[]{:S(2)}, u32[]{:S(2)}) collective-permute-start(f32[4,128,128]{2,1,0:T(8,128)} %transforms.2), channel_id=1, source_target_pairs={{0,3},{1,2},{2,1},{3,0},{4,7},{5,6},{6,5},{7,4},{8,11},{9,10},{10,... | collective-permute-start | bytes 786440 | tf_op jit(solution)/shard_map/ppermute | solution.py:553
  137.2 22.7 %collective-permute-start.5 = (f32[4,128,128]{2,1,0:T(8,128)}, f32[4,128,128]{2,1,0:T(8,128)}, u32[]{:S(2)}, u32[]{:S(2)}) collective-permute-start(f32[4,128,128]{2,1,0:T(8,128)} %transforms.2), channel_id=1, source_target_pairs={{0,2},{1,3},{2,0},{3,1},{4,6},{5,7},{6,4},{7,5},{8,10},{9,11},{10,... | collective-permute-start | bytes 786440 | tf_op jit(solution)/shard_map/ppermute | solution.py:553
  137.6 22.3 %collective-permute-start.4 = (f32[4,128,128]{2,1,0:T(8,128)}, f32[4,128,128]{2,1,0:T(8,128)}, u32[]{:S(2)}, u32[]{:S(2)}) collective-permute-start(f32[4,128,128]{2,1,0:T(8,128)} %transforms.2), channel_id=1, source_target_pairs={{0,1},{1,0},{2,3},{3,2},{4,5},{5,4},{6,7},{7,6},{8,9},{9,8},{10,11... | collective-permute-start | bytes 786440 | tf_op jit(solution)/shard_map/ppermute | solution.py:553
  181.5 1.6 copy-start.1
  191.3 16.4 %collective-permute-start.9 = (f32[9,64,256]{2,1,0:T(8,128)}, f32[9,64,256]{2,1,0:T(8,128)S(1)}, u32[]{:S(2)}, u32[]{:S(2)}) collective-permute-start(f32[9,64,256]{2,1,0:T(8,128)} %get-tuple-element.171), channel_id=1, source_target_pairs={{0,8},{1,9},{2,10},{3,11},{8,16},{9,17},{10,18},{11,19},{16,24},{1... | collective-permute-start | bytes 1769480 | tf_op jit(solution)/shard_map/ppermute | solution.py:550
  191.3 16.5 %collective-permute-start.10 = (f32[9,64,256]{2,1,0:T(8,128)}, f32[9,64,256]{2,1,0:T(8,128)S(1)}, u32[]{:S(2)}, u32[]{:S(2)}) collective-permute-start(f32[9,64,256]{2,1,0:T(8,128)} %get-tuple-element.172), channel_id=1, source_target_pairs={{0,4},{1,5},{2,6},{3,7},{8,0},{9,1},{10,2},{11,3},{16,8},{17,9},{1... | collective-permute-start | bytes 1769480 | tf_op jit(solution)/shard_map/ppermute | solution.py:550
  193.3 30.7 %collective-permute-start.7 = (f32[9,64,256]{2,1,0:T(8,128)}, f32[9,64,256]{2,1,0:T(8,128)S(1)}, u32[]{:S(2)}, u32[]{:S(2)}) collective-permute-start(f32[9,64,256]{2,1,0:T(8,128)} %get-tuple-element.166), channel_id=1, source_target_pairs={{0,8},{1,9},{2,10},{3,11},{8,16},{9,17},{10,18},{11,19},{16,24},{1... | collective-permute-start | bytes 1769480 | tf_op jit(solution)/shard_map/ppermute | solution.py:550
  193.3 30.6 %collective-permute-start.8 = (f32[9,64,256]{2,1,0:T(8,128)}, f32[9,64,256]{2,1,0:T(8,128)S(1)}, u32[]{:S(2)}, u32[]{:S(2)}) collective-permute-start(f32[9,64,256]{2,1,0:T(8,128)} %get-tuple-element.167), channel_id=1, source_target_pairs={{0,4},{1,5},{2,6},{3,7},{8,0},{9,1},{10,2},{11,3},{16,8},{17,9},{1... | collective-permute-start | bytes 1769480 | tf_op jit(solution)/shard_map/ppermute | solution.py:550
  207.7 1.0 copy-start.8
  223.9 16.9 %copy-start.9 = (f32[64,512]{1,0:T(8,128)S(1)}, f32[64,512]{1,0:T(8,128)}, u32[]{:S(2)}) copy-start(f32[64,512]{1,0:T(8,128)} %get-tuple-element.173) | copy-start | bytes 393220
  223.9 26.5 %copy-start.15 = (f32[4,128,2]{1,0,2:T(4,128)S(1)}, f32[4,128,2]{1,0,2:T(4,128)}, u32[]{:S(2)}) copy-start(f32[4,128,2]{1,0,2:T(4,128)} %copy-done.14) | copy-start | bytes 12292
  223.9 34.4 %copy-start.11 = (s32[4,128]{1,0:T(4,128)S(1)}, s32[4,128]{1,0:T(4,128)}, u32[]{:S(2)}) copy-start(s32[4,128]{1,0:T(4,128)} %copy-done.10) | copy-start | bytes 6148
  223.9 34.4 %copy-start.18 = (s32[32]{0:T(128)S(1)}, s32[32]{0:T(128)}, u32[]{:S(2)}) copy-start(s32[32]{0:T(128)} %constant.213.clone) | copy-start | bytes 388
  223.9 34.4 %copy-start.20 = (s32[5]{0:T(128)S(1)}, s32[5]{0:T(128)}, u32[]{:S(2)}) copy-start(s32[5]{0:T(128)} %copy-done.19) | copy-start | bytes 64
  223.9 34.4 %copy-start.22 = (s32[5]{0:T(128)S(1)}, s32[5]{0:T(128)}, u32[]{:S(2)}) copy-start(s32[5]{0:T(128)} %copy-done.21) | copy-start | bytes 64
  223.9 34.4 %copy-start.24 = (s32[5]{0:T(128)S(1)}, s32[5]{0:T(128)}, u32[]{:S(2)}) copy-start(s32[5]{0:T(128)} %copy-done.23) | copy-start | bytes 64
  223.9 34.4 %copy-start.26 = (s32[5]{0:T(128)S(1)}, s32[5]{0:T(128)}, u32[]{:S(2)}) copy-start(s32[5]{0:T(128)} %copy-done.25) | copy-start | bytes 64
  224.0 34.4 %copy-start.28 = (s32[5]{0:T(128)S(1)}, s32[5]{0:T(128)}, u32[]{:S(2)}) copy-start(s32[5]{0:T(128)} %copy-done.27) | copy-start | bytes 64
  242.1 4.3 %collective-permute-start.13 = (f32[128,128]{1,0:T(8,128)S(1)}, f32[128,128]{1,0:T(8,128)S(1)}, u32[]{:S(2)}, u32[]{:S(2)}) collective-permute-start(f32[128,128]{1,0:T(8,128)S(1)} %bitcast.152), channel_id=1, source_target_pairs={{0,3},{1,2},{2,1},{3,0},{4,7},{5,6},{6,5},{7,4},{8,11},{9,10},{10,... | collective-permute-start | bytes 196616 | tf_op jit(solution)/shard_map/ppermute | solution.py:553
  242.1 4.2 %collective-permute-start.11 = (f32[128,128]{1,0:T(8,128)S(1)}, f32[128,128]{1,0:T(8,128)S(1)}, u32[]{:S(2)}, u32[]{:S(2)}) collective-permute-start(f32[128,128]{1,0:T(8,128)S(1)} %bitcast.151), channel_id=1, source_target_pairs={{0,1},{1,0},{2,3},{3,2},{4,5},{5,4},{6,7},{7,6},{8,9},{9,8},{10,11... | collective-permute-start | bytes 196616 | tf_op jit(solution)/shard_map/ppermute | solution.py:553
  243.5 4.3 %collective-permute-start.12 = (f32[128,128]{1,0:T(8,128)S(1)}, f32[128,128]{1,0:T(8,128)S(1)}, u32[]{:S(2)}, u32[]{:S(2)}) collective-permute-start(f32[128,128]{1,0:T(8,128)S(1)} %bitcast.150), channel_id=1, source_target_pairs={{0,2},{1,3},{2,0},{3,1},{4,6},{5,7},{6,4},{7,5},{8,10},{9,11},{10,... | collective-permute-start | bytes 196616 | tf_op jit(solution)/shard_map/ppermute | solution.py:553
  247.8 5.6 %collective-permute-start.17 = (f32[128,128]{1,0:T(8,128)S(1)}, f32[128,128]{1,0:T(8,128)S(1)}, u32[]{:S(2)}, u32[]{:S(2)}) collective-permute-start(f32[128,128]{1,0:T(8,128)S(1)} %add_add_fusion), channel_id=1, source_target_pairs={{0,6},{1,7},{2,0},{3,1},{8,2},{9,3},{10,8},{11,9},{16,10},{17,11},... | collective-permute-start | bytes 196616 | tf_op jit(solution)/shard_map/ppermute | solution.py:550
  249.9 5.0 %collective-permute-start.16 = (f32[128,128]{1,0:T(8,128)S(1)}, f32[128,128]{1,0:T(8,128)S(1)}, u32[]{:S(2)}, u32[]{:S(2)}) collective-permute-start(f32[128,128]{1,0:T(8,128)S(1)} %add_add_fusion), channel_id=1, source_target_pairs={{0,7},{1,0},{2,1},{3,2},{8,3},{9,8},{10,9},{11,10},{16,11},{17,16}... | collective-permute-start | bytes 196616 | tf_op jit(solution)/shard_map/ppermute | solution.py:550
  249.9 5.0 %collective-permute-start.15 = (f32[128,128]{1,0:T(8,128)S(1)}, f32[128,128]{1,0:T(8,128)S(1)}, u32[]{:S(2)}, u32[]{:S(2)}) collective-permute-start(f32[128,128]{1,0:T(8,128)S(1)} %add_add_fusion), channel_id=1, source_target_pairs={{0,1},{1,2},{2,3},{3,8},{8,9},{9,10},{10,11},{11,16},{16,17},{17,1... | collective-permute-start | bytes 196616 | tf_op jit(solution)/shard_map/ppermute | solution.py:550
  250.4 7.9 %collective-permute-start.14 = (f32[128,128]{1,0:T(8,128)S(1)}, f32[128,128]{1,0:T(8,128)S(1)}, u32[]{:S(2)}, u32[]{:S(2)}) collective-permute-start(f32[128,128]{1,0:T(8,128)S(1)} %add_add_fusion), channel_id=1, source_target_pairs={{0,2},{1,3},{2,8},{3,9},{8,10},{9,11},{10,16},{11,17},{16,18},{17,... | collective-permute-start | bytes 196616 | tf_op jit(solution)/shard_map/ppermute | solution.py:550
  273.8 2.9 copy-start.3
  273.8 35.3 %all-to-all-start.5 = ((f32[32,1,4,8,256]{4,3,2,1,0:T(8,128)}), f32[32,1,4,8,256]{4,3,2,1,0:T(8,128)S(1)}, u32[]{:S(2)}, u32[]{:S(2)}) async-start(f32[32,1,4,8,256]{4,3,2,1,0:T(8,128)} %last_analysis.2), calls=%async_computation.5 | async-start | bytes 2097152 | tf_op jit(solution)/shard_map/all_to_all | solution.py:568
  276.7 17.0 %collective-permute-start.20 = (f32[4,128,128]{2,1,0:T(8,128)S(1)}, f32[4,128,128]{2,1,0:T(8,128)S(1)}, u32[]{:S(2)}, u32[]{:S(2)}) collective-permute-start(f32[4,128,128]{2,1,0:T(8,128)S(1)} %copy-done.3), channel_id=1, source_target_pairs={{0,3},{1,2},{2,1},{3,0},{4,7},{5,6},{6,5},{7,4},{8,11},{9,10},{10,... | collective-permute-start | bytes 786440 | tf_op jit(solution)/shard_map/ppermute | solution.py:553
  278.3 23.5 %collective-permute-start.19 = (f32[4,128,128]{2,1,0:T(8,128)S(1)}, f32[4,128,128]{2,1,0:T(8,128)S(1)}, u32[]{:S(2)}, u32[]{:S(2)}) collective-permute-start(f32[4,128,128]{2,1,0:T(8,128)S(1)} %copy-done.3), channel_id=1, source_target_pairs={{0,2},{1,3},{2,0},{3,1},{4,6},{5,7},{6,4},{7,5},{8,10},{9,11},{10,... | collective-permute-start | bytes 786440 | tf_op jit(solution)/shard_map/ppermute | solution.py:553
  278.7 23.1 %collective-permute-start.18 = (f32[4,128,128]{2,1,0:T(8,128)S(1)}, f32[4,128,128]{2,1,0:T(8,128)S(1)}, u32[]{:S(2)}, u32[]{:S(2)}) collective-permute-start(f32[4,128,128]{2,1,0:T(8,128)S(1)} %copy-done.3), channel_id=1, source_target_pairs={{0,1},{1,0},{2,3},{3,2},{4,5},{5,4},{6,7},{7,6},{8,9},{9,8},{10,11... | collective-permute-start | bytes 786440 | tf_op jit(solution)/shard_map/ppermute | solution.py:553
  309.1 76.1 %copy-start.2 = (f32[32,1,4,8,256]{4,3,2,1,0:T(8,128)}, f32[32,1,4,8,256]{4,3,2,1,0:T(8,128)S(1)}, u32[]{:S(2)}) copy-start(f32[32,1,4,8,256]{4,3,2,1,0:T(8,128)S(1)} %all-to-all-done.5.a_ref) | copy-start | bytes 3145732
  (7 other events, 4.7 us)
